TPU v7x, 128 devices: a whole 4x4x4 slice. The times are simulated.
128 devices in a mesh: ckpt: 8 (over x_lo, z), shard: 16 (over x_hi, y, core).
Axes of the slice: x: 4 (x_hi: 2, x_lo: 2; x = x_hi * 2 + x_lo), y: 4, z: 4, core: 2. Of those that a mesh axis runs over, the one named last changes fastest.
Arguments:
- task_vectors: bfloat16 [8, 4096, 16384], P('ckpt', 'shard'), may hold values from -0.125 to 0.125, as said below
- thresholds: float32 [8], replicated, may hold values from 0.009 to 0.062, as said below
- base_weight: float32 [4096, 16384], P('ckpt', 'shard'), may hold values from -0.3 to 0.3
Outputs:
- merged: float32 [4096, 16384], P('ckpt', 'shard')
Inputs may be any that keep to these rules, and one draw needn't show every extreme that they name: `task_vectors`: every entry is a whole multiple of 2^-14. `thresholds`: every threshold is an odd multiple of 2^-15.
All inputs are finite; a program needn't handle non-finite values.
Results may differ from a plain program's by a relative error of at most 0.0003.
Values may be sent and summed in bfloat16 or wider, within the bound.
No kernel may reach another device: no remote copies, remote signals or barrier semaphores. Data moves between devices by JAX's collectives and lax.ppermute only.
A program may use at most 128 MiB of HBM per device.

v0:
```python
import jax
import jax.numpy as jnp
from jax import lax
from jax.sharding import PartitionSpec as P


def in_blocks(array, dim, peers):
    shape = array.shape
    parts = array.reshape(*shape[:dim], peers, shape[dim] // peers, *shape[dim + 1 :])
    return jnp.moveaxis(parts, dim, 0)


def edges_of(length, count):
    unit = 8 if length >= 8 * count else 1
    return [length // unit * k // count * unit for k in range(1, count)]


def laid_out(parts, dim):
    shape = list(parts.shape[1:])
    shape[dim] *= parts.shape[0]
    return jnp.moveaxis(parts, 0, dim).reshape(shape)


def several_exchanges(array, axis, pieces, split_dim, concat_dim):
    parts = in_blocks(array, split_dim, lax.axis_size(axis))
    split_at = max(range(1, max(2, parts.ndim - 1)), key=lambda d: parts.shape[d])
    done = []
    for piece in jnp.split(parts, edges_of(parts.shape[split_at], pieces), axis=split_at):
        if piece.size:
            done.append(lax.all_to_all(piece, axis, split_axis=0, concat_axis=0, tiled=True))
    return laid_out(jnp.concatenate(done, axis=split_at), concat_dim)


def local_mean(all_tasks, limits):
    values = all_tasks.astype(jnp.float32)
    trimmed = jnp.where(jnp.abs(values) > limits[:, None, None], values, jnp.float32(0.0))
    signed_total = jnp.sum(trimmed, axis=0)
    agreeing = jnp.logical_or(
        jnp.logical_and(signed_total[None] > 0, trimmed > 0),
        jnp.logical_and(signed_total[None] < 0, trimmed < 0),
    )
    kept_sum = jnp.sum(jnp.where(agreeing, trimmed, jnp.float32(0.0)), axis=0)
    agree_count = jnp.sum(agreeing.astype(jnp.float32), axis=0)
    return jnp.where(agree_count > 0, kept_sum / jnp.maximum(agree_count, 1.0), jnp.float32(0.0))


def local(task_vectors, thresholds, base_weight):
    ckpt_count = lax.axis_size("ckpt")
    shard_count = lax.axis_size("shard")
    all_tasks = several_exchanges(task_vectors, "ckpt", 2, 1, 0)
    mean_part = local_mean(all_tasks, thresholds)
    block_rows = mean_part.shape[0]
    by_columns = lax.all_to_all(mean_part, "shard", split_axis=1, concat_axis=0, tiled=True)
    col_width = by_columns.shape[1]
    by_rows = lax.all_to_all(by_columns, "ckpt", split_axis=0, concat_axis=0, tiled=True)
    group_size = shard_count // ckpt_count
    disjoint = by_rows.reshape(ckpt_count, group_size, block_rows, col_width)
    disjoint = disjoint.transpose(1, 0, 2, 3).reshape(
        group_size * ckpt_count * block_rows, col_width
    )
    return base_weight + disjoint


def solution(mesh):
    placed = (P("ckpt", "shard", None), P(), P("ckpt", "shard"))
    return jax.shard_map(
        local, mesh=mesh, in_specs=placed, out_specs=P("ckpt", "shard"), check_vma=False
    )
```

profile of v0, /device:TPU:27, one launch (start us, length us, event | category | flops | bytes accessed | tf_op | source)
XLA Modules:
  0.0 189.8 jit_solution(17729370267367203730)
XLA Ops:
  0.0 3.9 %fusion.9 = (bf16[8,1,16,16384]{3,2,1,0:T(8,128)(2,1)S(1)}, bf16[8,1,16,16384]{3,2,1,0:T(8,128)(2,1)S(1)}) fusion(bf16[8,1,32,16384]{3,2,1,0:T(8,128)(2,1)} %bitcast.23), kind=kLoop, calls=%fused_computation.18 | loop fusion | bytes 16777216 | tf_op jit(solution)/shard_map/split | solution.py:28
  3.9 53.4 %all_to_all.32 = bf16[8,1,16,16384]{3,2,1,0:T(8,128)(2,1)S(1)} all-to-all(bf16[8,1,16,16384]{3,2,1,0:T(8,128)(2,1)S(1)} %get-tuple-element.7), channel_id=1, replica_groups=mesh['ckpt'=8,'shard'=16] {'ckpt'}, dimensions={0} | all-to-all | bytes 8388608 | tf_op jit(solution)/shard_map/all_to_all | solution.py:30
  57.3 0.0 copy-start.1
  57.3 49.4 %all_to_all.33 = bf16[8,1,16,16384]{3,2,1,0:T(8,128)(2,1)S(1)} all-to-all(bf16[8,1,16,16384]{3,2,1,0:T(8,128)(2,1)S(1)} %get-tuple-element.8), channel_id=1, replica_groups=mesh['ckpt'=8,'shard'=16] {'ckpt'}, dimensions={0} | all-to-all | bytes 8388608 | tf_op jit(solution)/shard_map/all_to_all | solution.py:30
  106.7 0.0 copy-done.1
  106.7 4.1 %fusion.3 = f32[32,16384]{1,0:T(8,128)S(1)} fusion(f32[8]{0:T(128)S(1)} %copy-done.1, bf16[8,1,16,16384]{3,2,1,0:T(8,128)(2,1)S(1)} %all_to_all.33, bf16[8,1,16,16384]{3,2,1,0:T(8,128)(2,1)S(1)} %all_to_all.32), kind=kLoop, calls=%fused_computation.5 | loop fusion | flops 37224448 | bytes 10485792 | tf_op jit(solution)/shard_map/reduce_sum | solution.py:37
  110.8 0.5 broadcast_compare_fusion.1
  111.3 9.5 %convert_reduce_fusion = (f32[32,16384]{1,0:T(8,128)S(1)}, f32[32,16384]{1,0:T(8,128)S(1)}) fusion(f32[8]{0:T(128)S(1)} %copy-done.1, bf16[8,1,16,16384]{3,2,1,0:T(8,128)(2,1)S(1)} %all_to_all.33, bf16[8,1,16,16384]{3,2,1,0:T(8,128)(2,1)S(1)} %all_to_all.32, pred[32,16384]{1,0:T(8,128)(4,1)S(1)} %get-tuple-element.10, pred[32,16384]{1,0:T(8,128)(4,1)S(1)} %get-tuple-element.9), kind=kLoop, calls=%fused_computation.8 | loop fusion | flops 70254592 | bytes 13631520 | tf_op jit(solution)/shard_map/reduce_sum | solution.py:43
  120.9 0.3 divide_select_fusion
  121.2 0.2 copy.10
  121.5 36.9 %all_to_all.34 = f32[32,16,1024]{2,0,1:T(8,128)S(1)} all-to-all(f32[32,16,1024]{2,0,1:T(8,128)S(1)} %bitcast.24), channel_id=1, replica_groups=mesh['ckpt'=8,'shard'=16] {'shard'}, dimensions={1} | all-to-all | bytes 4194304 | tf_op jit(solution)/shard_map/all_to_all | solution.py:53
  158.4 0.0 copy-start
  158.4 29.4 %all_to_all.35 = f32[8,64,1024]{2,1,0:T(8,128)S(1)} all-to-all(f32[8,64,1024]{2,1,0:T(8,128)S(1)} %bitcast.25), channel_id=1, replica_groups=mesh['ckpt'=8,'shard'=16] {'ckpt'}, dimensions={0} | all-to-all | bytes 4194304 | tf_op jit(solution)/shard_map/all_to_all | solution.py:55
  187.8 0.2 copy.7
  188.1 0.0 copy-done
  188.1 1.7 bitcast_add_fusion
Async XLA Ops:
  57.3 49.4 %copy-start.1 = (f32[8]{0:T(128)S(1)}, f32[8]{0:T(128)}, u32[]{:S(2)}) copy-start(f32[8]{0:T(128)} %param.4) | copy-start | bytes 100
  158.4 29.7 %copy-start = (f32[512,1024]{1,0:T(8,128)S(1)}, f32[512,1024]{1,0:T(8,128)}, u32[]{:S(2)}) copy-start(f32[512,1024]{1,0:T(8,128)} %param.5) | copy-start | bytes 6291460
where the time goes:
time: 193 us; the launch traced here: 190 us
  blocking collectives  169 us (88%)
  other arithmetic  16.2 us (8%)
  local copies, waits for them, and re-layouts  4.38 us (2%)
    all_to_all x2, blocking collectives, several_exchanges(): lax.all_to_all(piece, axis, split_axis=0, concat_axis=0, tiled=True)  103 us
    all_to_all x1, blocking collectives, local(): lax.all_to_all(mean_part, 'shard', split_axis=1, concat_axis=0, tiled=True)  36.9 us
    all_to_all x1, blocking collectives, local(): lax.all_to_all(by_columns, 'ckpt', split_axis=0, concat_axis=0, tiled=True)  29.4 us
    reduce_sum x1, other arithmetic, local_mean(): agree_count = jnp.sum(agreeing.astype(jnp.float32), axis=0)  9.54 us
    reduce_sum x1, other arithmetic, local_mean(): signed_total = jnp.sum(trimmed, axis=0)  4.06 us
    split x1, local copies, waits for them, and re-layouts, several_exchanges(): jnp.split(parts, edges_of(parts.shape[split_at], pieces), axis=split_at)  3.9 us

commit v1 on v0

v1 whole, which is shorter than its diff:
```python
import functools

import jax
import jax.numpy as jnp
from jax import lax
from jax.experimental import pallas as pl
from jax.experimental.pallas import tpu as pltpu
from jax.sharding import PartitionSpec as P

AXES = ("ckpt", "shard")
CHUNKS = (208, 48)
LIFT = 4.0
SCALE, SHIFT = 1920.0, -120.0
BLOCK_ROWS = 16
SLICE = 128


def number(x, y, z, c):
    return ((x % 2) * 4 + z % 4) * 16 + ((x // 2) * 4 + y % 4) * 2 + c


PLACES = [(x, y, z, c) for x in range(4) for y in range(4) for z in range(4) for c in range(2)]


def pairs(target):
    return [(number(*p), number(*target(*p))) for p in PLACES]


def column_x(x_lo, c):
    return x_lo ^ c


def column_y(y, z, c):
    return (z - y + 2 * c + 4) % 4


def home(half):
    return lambda x, y, z, c: (x // 2 + 2 * column_x(x % 2, c), column_y(y, z, c), y, c ^ half)


def pack_kernel(at, order, own, out, sems):
    count, rows, width = out.shape
    copies = []
    for i in range(count):
        column = pl.multiple_of(order[i] * width, width)
        copies.append(pltpu.make_async_copy(own.at[pl.ds(at, rows), pl.ds(column, width)], out.at[i], sems.at[i]))
    for copy in copies:
        copy.start()
    for copy in copies:
        copy.wait()


def packed(own, order, at, rows):
    width = own.shape[1] // 8
    return pl.pallas_call(
        functools.partial(pack_kernel, at),
        in_specs=[pl.BlockSpec(memory_space=pltpu.SMEM), pl.BlockSpec(memory_space=pltpu.HBM)],
        out_specs=pl.BlockSpec(memory_space=pl.ANY),
        scratch_shapes=[pltpu.SemaphoreType.DMA((8,))],
        out_shape=OUT((8, rows, width), own.dtype),
        compiler_params=pltpu.CompilerParams(vmem_limit_bytes=2**20),
        name="pack",
    )(order, own)


OUT = jax.ShapeDtypeStruct


def coded(mean):
    size = jnp.exp2(jnp.abs(mean) * SCALE + SHIFT)
    return jnp.where(mean < 0, -size, size).astype(jnp.bfloat16)


def decoded(code):
    code = code.astype(jnp.float32)
    size = jnp.abs(code)
    mean = (jnp.log2(size) - SHIFT) * (1.0 / SCALE)
    mean = jnp.where(size > 2.0 ** (SHIFT + 1), mean, 0.0)
    return jnp.where(code < 0, -mean, mean)


def mean_kernel(core, limits, tasks_same, tasks_other, same, other):
    for tasks, out in ((tasks_same, same), (tasks_other, other)):
        for first in range(0, out.shape[1], SLICE):
            high = jnp.zeros((BLOCK_ROWS, SLICE), jnp.float32)
            low = jnp.zeros((BLOCK_ROWS, SLICE), jnp.float32)
            for t in range(8):
                value = tasks[t, :, first : first + SLICE].astype(jnp.float32)
                limit = limits[t]
                high = high + jnp.where(value > limit, value + LIFT, 0.0)
                low = low + jnp.where(value < -limit, value - LIFT, 0.0)
            high_count = jnp.floor(high * (1.0 / LIFT))
            low_count = jnp.floor(low * (-1.0 / LIFT))
            high_sum = high - LIFT * high_count
            low_sum = low + LIFT * low_count
            total = high_sum + low_sum
            kept = jnp.where(total > 0, high_sum, low_sum)
            count = jnp.where(total > 0, high_count, low_count)
            mean = jnp.where(total != 0, kept / jnp.maximum(count, 1.0), 0.0)
            out[:, first : first + SLICE] = coded(mean)


def disjoint_mean(tasks, limits, core):
    count, rows, width = tasks.shape
    out = jax.ShapeDtypeStruct((rows, width // 2), jnp.bfloat16)
    block = pl.BlockSpec((BLOCK_ROWS, width // 2), lambda r, *_: (r, 0))
    return pl.pallas_call(
        mean_kernel,
        grid_spec=pltpu.PrefetchScalarGridSpec(
            num_scalar_prefetch=2,
            grid=(rows // BLOCK_ROWS,),
            in_specs=[
                pl.BlockSpec((count, BLOCK_ROWS, width // 2), lambda r, core, limits: (0, r, core[0])),
                pl.BlockSpec((count, BLOCK_ROWS, width // 2), lambda r, core, limits: (0, r, 1 - core[0])),
            ],
            out_specs=[block, block],
        ),
        out_shape=[out, out],
        compiler_params=pltpu.CompilerParams(vmem_limit_bytes=16 * 2**20),
        name="mean",
    )(core, limits, tasks, tasks)


def local(task_vectors, thresholds, base_weight):
    own = task_vectors[0]
    shard = lax.axis_index("shard")
    y, c = (shard // 2) % 4, shard % 2
    core = c[None].astype(jnp.int32)
    place = jnp.arange(8, dtype=jnp.int32)
    order = column_x(place // 4, c) * 4 + column_y(y, place % 4, c)
    at, same, other = 0, [], []
    for rows in CHUNKS:
        blocks = packed(own, order, at, rows)
        tasks = lax.all_to_all(blocks, "ckpt", split_axis=0, concat_axis=0, tiled=True)
        code_same, code_other = disjoint_mean(tasks, thresholds, core)
        same.append(lax.ppermute(code_same, AXES, pairs(home(0))))
        other.append(lax.ppermute(code_other, AXES, pairs(home(1))))
        at += rows
    same, other = jnp.concatenate(same), jnp.concatenate(other)
    first = jnp.where(c == 0, same, other)
    second = jnp.where(c == 0, other, same)
    return base_weight + decoded(jnp.concatenate([first, second]))


def solution(mesh):
    placed = (P("ckpt", "shard", None), P(), P("ckpt", "shard"))
    return jax.shard_map(
        local, mesh=mesh, in_specs=placed, out_specs=P("ckpt", "shard"), check_vma=False
    )
```

time: 193 us -> 143 us (0.74)
  the two profiles are of different devices: /device:TPU:27 before, /device:TPU:30 now
where the time goes in v1:
time: 143 us
  waiting for transfers between devices  89.6 us (63%)
  starting transfers between devices  24.9 us (17%)
  Pallas kernels  16.1 us (11%)
  local copies, waits for them, and re-layouts  9.72 us (7%)
  other arithmetic  2.3 us (2%)
    all_to_all x2, waiting for transfers between devices, local(): lax.all_to_all(blocks, 'ckpt', split_axis=0, concat_axis=0, tiled=True)  82.3 us
    pallas_call x2, Pallas kernels, disjoint_mean(): pl.pallas_call(mean_kernel, grid_spec=pltpu.PrefetchScalarGridSpec(num_sc...  13 us
    all_to_all x2, starting transfers between devices, local(): lax.all_to_all(blocks, 'ckpt', split_axis=0, concat_axis=0, tiled=True)  11 us
    unnamed x12, local copies, waits for them, and re-layouts  9.7 us
    ppermute x2, waiting for transfers between devices, local(): same.append(lax.ppermute(code_same, AXES, pairs(home(0))))  7.18 us
    ppermute x2, starting transfers between devices, local(): other.append(lax.ppermute(code_other, AXES, pairs(home(1))))  6.99 us
    ppermute x2, starting transfers between devices, local(): same.append(lax.ppermute(code_same, AXES, pairs(home(0))))  6.9 us
    pallas_call x2, Pallas kernels, packed(): pl.pallas_call(functools.partial(pack_kernel, at), in_specs=[pl.BlockSpec...  3.11 us
  transfers between devices with their start and end apart: 6, of which 4 were waited for; matrix products, arithmetic and copies ran while one was open for 0% of the time, Pallas kernels for 10%

profile of v1, /device:TPU:30, one launch (start us, length us, event | category | flops | bytes accessed | tf_op | source)
XLA Modules:
  0.0 142.8 jit_solution(4957719574240700290)
XLA Ops:
  0.0 3.4 %copy-done = bf16[1,256,16384]{2,1,0:T(8,128)(2,1)S(1)} copy-done((bf16[1,256,16384]{2,1,0:T(8,128)(2,1)S(1)}, bf16[1,256,16384]{2,1,0:T(8,128)(2,1)}, u32[]{:S(2)}) %copy-start) | copy-done | bytes 8388632
  3.4 1.4 pack.2
  4.8 0.0 copy-start.2
  4.8 2.9 %copy-done.2 = bf16[8,208,2048]{2,1,0:T(8,128)(2,1)} copy-done((bf16[8,208,2048]{2,1,0:T(8,128)(2,1)}, bf16[8,208,2048]{2,1,0:T(8,128)(2,1)S(1)}, u32[]{:S(2)}) %copy-start.2) | copy-done | bytes 6815768
  7.7 6.8 %all-to-all-start = ((bf16[8,208,2048]{2,1,0:T(8,128)(2,1)}), bf16[8,208,2048]{2,1,0:T(8,128)(2,1)}, u32[]{:S(2)}, u32[]{:S(2)}) async-start(bf16[8,208,2048]{2,1,0:T(8,128)(2,1)} %copy-done.2), calls=%async_computation | async-start | bytes 13631488 | tf_op jit(solution)/shard_map/all_to_all | solution.py:134
  14.4 3.4 %copy-done.1 = bf16[1,256,16384]{2,1,0:T(8,128)(2,1)S(1)} copy-done((bf16[1,256,16384]{2,1,0:T(8,128)(2,1)S(1)}, bf16[1,256,16384]{2,1,0:T(8,128)(2,1)}, u32[]{:S(2)}) %copy-start.1) | copy-done | bytes 8388632
  17.8 1.7 %pack.3 = bf16[8,48,2048]{2,1,0:T(8,128)(2,1)} custom-call(s32[8]{0:T(128)S(1)} %fusion.10.order, bf16[256,16384]{1,0:T(8,128)(2,1)S(1)} %bitcast.3), custom_call_target="tpu_custom_call" | custom-call | tf_op jit(solution)/shard_map/pack/pallas_call | solution.py:55
  19.6 0.0 copy-start.3
  19.6 71.0 %all-to-all-done.tasks_same.tasks_other = bf16[8,208,2048]{2,1,0:T(8,128)(2,1)} async-done(((bf16[8,208,2048]{2,1,0:T(8,128)(2,1)}), bf16[8,208,2048]{2,1,0:T(8,128)(2,1)}, u32[]{:S(2)}, u32[]{:S(2)}) %all-to-all-start) | async-done | bytes 6815776 | tf_op jit(solution)/shard_map/all_to_all | solution.py:134
  90.6 4.2 %all-to-all-start.1 = ((bf16[8,48,2048]{2,1,0:T(8,128)(2,1)}), bf16[8,48,2048]{2,1,0:T(8,128)(2,1)S(1)}, u32[]{:S(2)}, u32[]{:S(2)}) async-start(bf16[8,48,2048]{2,1,0:T(8,128)(2,1)} %pack.3), calls=%async_computation.1 | async-start | bytes 3145728 | tf_op jit(solution)/shard_map/all_to_all | solution.py:134
  94.8 0.0 copy-done.3
  94.8 11.0 %mean.2 = (bf16[208,1024]{1,0:T(8,128)(2,1)S(1)}, bf16[208,1024]{1,0:T(8,128)(2,1)S(1)}) custom-call(s32[1]{0:T(128)} %bitcast.core, f32[8]{0:T(128)S(1)} %copy-done.3, bf16[8,208,2048]{2,1,0:T(8,128)(2,1)} %all-to-all-done.tasks_same.tasks_other, bf16[8,208,2048]{2,1,0:T(8,128)(2,1)} %all-to-all-done.tasks_same.tasks_other), custom_call_target="tpu_custom_call" | custom-call | tf_op jit(solution)/shard_map/mean/pallas_call | solution.py:107
  105.8 2.6 %collective-permute-start.2 = (bf16[208,1024]{1,0:T(8,128)(2,1)S(1)}, bf16[208,1024]{1,0:T(8,128)(2,1)S(1)}, u32[]{:S(2)}, u32[]{:S(2)}) collective-permute-start(bf16[208,1024]{1,0:T(8,128)(2,1)S(1)} %get-tuple-element.11), channel_id=1, source_target_pairs={{0,1},{1,12},{16,3},{17,14},{32,5},{33,8},{48,7},{49,10},{2,23},{3... | collective-permute-start | bytes 1277960 | tf_op jit(solution)/shard_map/ppermute | solution.py:137
  108.4 4.4 %collective-permute-start = (bf16[208,1024]{1,0:T(8,128)(2,1)S(1)}, bf16[208,1024]{1,0:T(8,128)(2,1)S(1)}, u32[]{:S(2)}, u32[]{:S(2)}) collective-permute-start(bf16[208,1024]{1,0:T(8,128)(2,1)S(1)} %get-tuple-element.9), channel_id=1, source_target_pairs={{0,0},{1,13},{16,2},{17,15},{32,4},{33,9},{48,6},{49,11},{2,22},{3... | collective-permute-start | bytes 1277960 | tf_op jit(solution)/shard_map/ppermute | solution.py:136
  112.8 11.3 %all-to-all-done.1.tasks_same.tasks_other = bf16[8,48,2048]{2,1,0:T(8,128)(2,1)S(1)} async-done(((bf16[8,48,2048]{2,1,0:T(8,128)(2,1)}), bf16[8,48,2048]{2,1,0:T(8,128)(2,1)S(1)}, u32[]{:S(2)}, u32[]{:S(2)}) %all-to-all-start.1) | async-done | bytes 1572896 | tf_op jit(solution)/shard_map/all_to_all | solution.py:134
  124.1 2.1 %mean.3 = (bf16[48,1024]{1,0:T(8,128)(2,1)S(1)}, bf16[48,1024]{1,0:T(8,128)(2,1)S(1)}) custom-call(s32[1]{0:T(128)} %bitcast.core, f32[8]{0:T(128)S(1)} %copy-done.3, bf16[8,48,2048]{2,1,0:T(8,128)(2,1)S(1)} %all-to-all-done.1.tasks_same.tasks_other, bf16[8,48,2048]{2,1,0:T(8,128)(2,1)S(1)} %all-to-all-done.1.tasks_same.tasks_other), custom_call_target="tpu_custom_call" | custom-call | tf_op jit(solution)/shard_map/mean/pallas_call | solution.py:107
  126.2 4.4 %collective-permute-start.3 = (bf16[48,1024]{1,0:T(8,128)(2,1)S(1)}, bf16[48,1024]{1,0:T(8,128)(2,1)S(1)}, u32[]{:S(2)}, u32[]{:S(2)}) collective-permute-start(bf16[48,1024]{1,0:T(8,128)(2,1)S(1)} %get-tuple-element.12), channel_id=1, source_target_pairs={{0,1},{1,12},{16,3},{17,14},{32,5},{33,8},{48,7},{49,10},{2,23},{3... | collective-permute-start | bytes 294920 | tf_op jit(solution)/shard_map/ppermute | solution.py:137
  130.5 2.5 %collective-permute-start.1 = (bf16[48,1024]{1,0:T(8,128)(2,1)S(1)}, bf16[48,1024]{1,0:T(8,128)(2,1)S(1)}, u32[]{:S(2)}, u32[]{:S(2)}) collective-permute-start(bf16[48,1024]{1,0:T(8,128)(2,1)S(1)} %get-tuple-element.10), channel_id=1, source_target_pairs={{0,0},{1,13},{16,2},{17,15},{32,4},{33,9},{48,6},{49,11},{2,22},{3... | collective-permute-start | bytes 294920 | tf_op jit(solution)/shard_map/ppermute | solution.py:136
  133.1 0.0 collective-permute-done.2
  133.1 0.0 collective-permute-done
  133.2 0.1 collective-permute-done.3
  133.3 7.2 %collective-permute-done.1 = bf16[48,1024]{1,0:T(8,128)(2,1)S(1)} collective-permute-done((bf16[48,1024]{1,0:T(8,128)(2,1)S(1)}, bf16[48,1024]{1,0:T(8,128)(2,1)S(1)}, u32[]{:S(2)}, u32[]{:S(2)}) %collective-permute-start.1) | collective-permute-done | bytes 98336 | tf_op jit(solution)/shard_map/ppermute | solution.py:136
  140.5 0.1 broadcast_select_fusion.1
  140.6 2.2 %fusion.6 = f32[512,1024]{1,0:T(8,128)} fusion(f32[512,1024]{1,0:T(8,128)S(1)} %copy-done.4, bf16[256,1024]{1,0:T(8,128)(2,1)S(1)} %get-tuple-element.14, bf16[256,1024]{1,0:T(8,128)(2,1)S(1)} %get-tuple-element.13), kind=kLoop, calls=%fused_computation.9 | loop fusion | flops 7340032 | bytes 5242880 | tf_op jit(solution)/shard_map/add | solution.py:142
  (9 shorter events, 0.1 us)
Async XLA Ops:
  0.0 3.4 %copy-start = (bf16[1,256,16384]{2,1,0:T(8,128)(2,1)S(1)}, bf16[1,256,16384]{2,1,0:T(8,128)(2,1)}, u32[]{:S(2)}) copy-start(bf16[1,256,16384]{2,1,0:T(8,128)(2,1)} %param.3) | copy-start | bytes 25165828
  4.8 2.9 %copy-start.2 = (bf16[8,208,2048]{2,1,0:T(8,128)(2,1)}, bf16[8,208,2048]{2,1,0:T(8,128)(2,1)S(1)}, u32[]{:S(2)}) copy-start(bf16[8,208,2048]{2,1,0:T(8,128)(2,1)S(1)} %pack.2) | copy-start | bytes 20447236
  7.7 82.9 %all-to-all-start = ((bf16[8,208,2048]{2,1,0:T(8,128)(2,1)}), bf16[8,208,2048]{2,1,0:T(8,128)(2,1)}, u32[]{:S(2)}, u32[]{:S(2)}) async-start(bf16[8,208,2048]{2,1,0:T(8,128)(2,1)} %copy-done.2), calls=%async_computation | async-start | bytes 13631488 | tf_op jit(solution)/shard_map/all_to_all | solution.py:134
  14.4 3.4 %copy-start.1 = (bf16[1,256,16384]{2,1,0:T(8,128)(2,1)S(1)}, bf16[1,256,16384]{2,1,0:T(8,128)(2,1)}, u32[]{:S(2)}) copy-start(bf16[1,256,16384]{2,1,0:T(8,128)(2,1)} %param.3) | copy-start | bytes 25165828
  19.6 75.2 %copy-start.3 = (f32[8]{0:T(128)S(1)}, f32[8]{0:T(128)}, u32[]{:S(2)}) copy-start(f32[8]{0:T(128)} %limits.3) | copy-start | bytes 100
  90.6 33.6 %all-to-all-start.1 = ((bf16[8,48,2048]{2,1,0:T(8,128)(2,1)}), bf16[8,48,2048]{2,1,0:T(8,128)(2,1)S(1)}, u32[]{:S(2)}, u32[]{:S(2)}) async-start(bf16[8,48,2048]{2,1,0:T(8,128)(2,1)} %pack.3), calls=%async_computation.1 | async-start | bytes 3145728 | tf_op jit(solution)/shard_map/all_to_all | solution.py:134
  105.8 27.3 %collective-permute-start.2 = (bf16[208,1024]{1,0:T(8,128)(2,1)S(1)}, bf16[208,1024]{1,0:T(8,128)(2,1)S(1)}, u32[]{:S(2)}, u32[]{:S(2)}) collective-permute-start(bf16[208,1024]{1,0:T(8,128)(2,1)S(1)} %get-tuple-element.11), channel_id=1, source_target_pairs={{0,1},{1,12},{16,3},{17,14},{32,5},{33,8},{48,7},{49,10},{2,23},{3... | collective-permute-start | bytes 1277960 | tf_op jit(solution)/shard_map/ppermute | solution.py:137
  108.4 24.7 %collective-permute-start = (bf16[208,1024]{1,0:T(8,128)(2,1)S(1)}, bf16[208,1024]{1,0:T(8,128)(2,1)S(1)}, u32[]{:S(2)}, u32[]{:S(2)}) collective-permute-start(bf16[208,1024]{1,0:T(8,128)(2,1)S(1)} %get-tuple-element.9), channel_id=1, source_target_pairs={{0,0},{1,13},{16,2},{17,15},{32,4},{33,9},{48,6},{49,11},{2,22},{3... | collective-permute-start | bytes 1277960 | tf_op jit(solution)/shard_map/ppermute | solution.py:136
  126.2 7.1 %collective-permute-start.3 = (bf16[48,1024]{1,0:T(8,128)(2,1)S(1)}, bf16[48,1024]{1,0:T(8,128)(2,1)S(1)}, u32[]{:S(2)}, u32[]{:S(2)}) collective-permute-start(bf16[48,1024]{1,0:T(8,128)(2,1)S(1)} %get-tuple-element.12), channel_id=1, source_target_pairs={{0,1},{1,12},{16,3},{17,14},{32,5},{33,8},{48,7},{49,10},{2,23},{3... | collective-permute-start | bytes 294920 | tf_op jit(solution)/shard_map/ppermute | solution.py:137
  130.5 10.0 %copy-start.4 = (f32[512,1024]{1,0:T(8,128)S(1)}, f32[512,1024]{1,0:T(8,128)}, u32[]{:S(2)}) copy-start(f32[512,1024]{1,0:T(8,128)} %param.5) | copy-start | bytes 6291460
  130.5 9.9 %collective-permute-start.1 = (bf16[48,1024]{1,0:T(8,128)(2,1)S(1)}, bf16[48,1024]{1,0:T(8,128)(2,1)S(1)}, u32[]{:S(2)}, u32[]{:S(2)}) collective-permute-start(bf16[48,1024]{1,0:T(8,128)(2,1)S(1)} %get-tuple-element.10), channel_id=1, source_target_pairs={{0,0},{1,13},{16,2},{17,15},{32,4},{33,9},{48,6},{49,11},{2,22},{3... | collective-permute-start | bytes 294920 | tf_op jit(solution)/shard_map/ppermute | solution.py:136

commit v2 on v1

v2 whole, which is shorter than its diff:
```python
import functools

import jax
import jax.numpy as jnp
from jax import lax
from jax.experimental import pallas as pl
from jax.experimental.pallas import tpu as pltpu
from jax.sharding import Mesh, PartitionSpec as P

SIZES = dict(x_lo=2, z=4, x_hi=2, y=4, core=2)
AXES = tuple(SIZES)
CHUNKS = (192, 64)
STEPS = ((1, 0), (3, 1), (2, 0), (1, 1), (3, 0), (2, 1), (0, 1))
EARLY, GATE_ON = (5,), 4
AHEAD = 8
LIFT = 4.0
SCALE, SHIFT = 1920.0, -120.0
BLOCK_ROWS, ADD_ROWS = 64, 64
TILE_ROWS, SLICE = 16, 128


def columns_of(x_lo, y, z, core):
    return x_lo, (z - y + 2 * core + 4) % 4


def moved(x_lo, z, core, hops, flip):
    return x_lo ^ flip, (z + hops * (1 - 2 * core) + 4) % 4


def meet(hops, flip):
    def target(x_lo, z, x_hi, y, core):
        return *moved(x_lo, z, core, hops, flip), x_hi, y, core

    return target


def home(half):
    def target(x_lo, z, x_hi, y, core):
        return x_hi, y, *columns_of(x_lo, y, z, core), core ^ half

    return target


def number(place):
    at = 0
    for index, size in zip(place, SIZES.values()):
        at = at * size + index
    return at


def pairs(target):
    places = [()]
    for size in SIZES.values():
        places = [place + (index,) for place in places for index in range(size)]
    return [(number(place), number(target(*place))) for place in places]


def pack_kernel(at, order, own, out, held, came, went):
    count, rows, width = out.shape
    loads, stores = [], []
    for i in range(count):
        column = pl.multiple_of(order[i] * width, width)
        loads.append(pltpu.make_async_copy(own.at[pl.ds(at, rows), pl.ds(column, width)], held.at[i], came.at[i]))
        stores.append(pltpu.make_async_copy(held.at[i], out.at[i], went.at[i]))
    for load in loads[:AHEAD]:
        load.start()
    for i, (load, store) in enumerate(zip(loads, stores)):
        load.wait()
        store.start()
        if i + AHEAD < count:
            loads[i + AHEAD].start()
    for store in stores:
        store.wait()


def packed(own, order, at, rows):
    count = order.shape[0]
    shape = (count, rows, own.shape[1] // count)
    return pl.pallas_call(
        functools.partial(pack_kernel, at),
        in_specs=[pl.BlockSpec(memory_space=pltpu.SMEM), pl.BlockSpec(memory_space=pl.ANY)],
        out_specs=pl.BlockSpec(memory_space=pl.ANY),
        scratch_shapes=[
            pltpu.VMEM(shape, own.dtype),
            pltpu.SemaphoreType.DMA((count,)),
            pltpu.SemaphoreType.DMA((count,)),
        ],
        out_shape=jax.ShapeDtypeStruct(shape, own.dtype),
        compiler_params=pltpu.CompilerParams(vmem_limit_bytes=60 * 2**20),
        name="pack",
    )(order, own)


def coded(mean):
    size = jnp.exp2(jnp.abs(mean) * SCALE + SHIFT)
    return jnp.where(mean < 0, -size, size).astype(jnp.bfloat16)


def decoded(code):
    code = code.astype(jnp.float32)
    size = jnp.abs(code)
    mean = (jnp.log2(size) - SHIFT) * (1.0 / SCALE)
    mean = jnp.where(size > 2.0 ** (SHIFT + 1), mean, 0.0)
    return jnp.where(code < 0, -mean, mean)


def merged_tile(values, limits):
    high = low = None
    for value, limit in zip(values, limits):
        lifted = value + LIFT
        above = jnp.where(value > limit, lifted, 0.0)
        below = jnp.where(value < -limit, lifted, 0.0)
        high = above if high is None else high + above
        low = below if low is None else low + below
    high_count = jnp.floor(high * (1.0 / LIFT))
    low_count = jnp.ceil(low * (1.0 / LIFT))
    high_sum = high - LIFT * high_count
    low_sum = low - LIFT * low_count
    total = high_sum + low_sum
    kept = jnp.where(total > 0, high_sum, low_sum)
    count = jnp.where(total > 0, high_count, low_count)
    return jnp.where(total != 0, kept / jnp.maximum(count, 1.0), 0.0)


def mean_kernel(core, limits, tasks_same, tasks_other, same, other):
    for tasks, out in ((tasks_same, same), (tasks_other, other)):
        for row in range(0, out.shape[0], TILE_ROWS):
            for column in range(0, out.shape[1], SLICE):
                tile = pl.ds(row, TILE_ROWS), pl.ds(column, SLICE)
                values = [tasks[(t, *tile)].astype(jnp.float32) for t in range(tasks.shape[0])]
                out[tile] = coded(merged_tile(values, [limits[t] for t in range(len(values))]))


def coded_mean(tasks, limits, core):
    count, rows, width = tasks.shape
    out = jax.ShapeDtypeStruct((rows, width // 2), jnp.bfloat16)
    block = pl.BlockSpec((BLOCK_ROWS, width // 2), lambda r, *_: (r, 0))
    half = (count, BLOCK_ROWS, width // 2)
    return pl.pallas_call(
        mean_kernel,
        grid_spec=pltpu.PrefetchScalarGridSpec(
            num_scalar_prefetch=2,
            grid=(rows // BLOCK_ROWS,),
            in_specs=[
                pl.BlockSpec(half, lambda r, core, limits: (0, r, core[0])),
                pl.BlockSpec(half, lambda r, core, limits: (0, r, 1 - core[0])),
            ],
            out_specs=[block, block],
        ),
        out_shape=[out, out],
        compiler_params=pltpu.CompilerParams(vmem_limit_bytes=16 * 2**20),
        name="mean",
    )(core, limits, tasks, tasks)


def blocks_kernel(core, source, thresholds, *refs):
    blocks, outs = refs[:8], refs[8:]
    width = outs[0].shape[1]
    limits = [thresholds[source[i]] for i in range(8)]
    for half, out in enumerate(outs):
        for row in range(0, out.shape[0], TILE_ROWS):
            for first in range(0, width, SLICE):
                at = pl.multiple_of((core[0] ^ half) * width + first, SLICE)
                values = [block[pl.ds(row, TILE_ROWS), pl.ds(at, SLICE)].astype(jnp.float32) for block in blocks]
                out[pl.ds(row, TILE_ROWS), pl.ds(first, SLICE)] = coded(merged_tile(values, limits))


def coded_mean_of(blocks, source, thresholds, core):
    rows, width = blocks[0].shape
    out = jax.ShapeDtypeStruct((rows, width // 2), jnp.bfloat16)
    unit = min(rows, BLOCK_ROWS)
    block = pl.BlockSpec((unit, width), lambda r, *_: (r, 0))
    return pl.pallas_call(
        blocks_kernel,
        grid_spec=pltpu.PrefetchScalarGridSpec(
            num_scalar_prefetch=3,
            grid=(rows // unit,),
            in_specs=[block] * 8,
            out_specs=[pl.BlockSpec((unit, width // 2), lambda r, *_: (r, 0))] * 2,
        ),
        out_shape=[out, out],
        compiler_params=pltpu.CompilerParams(vmem_limit_bytes=16 * 2**20),
        name="mean_of_blocks",
    )(core, source, thresholds, *blocks)


def add_kernel(core, base, same, other, *rest):
    out = rest[-1]

    @pl.when(pl.program_id(0) == 0)
    def _():
        out[...] = base[...] + decoded(same[...])

    @pl.when(pl.program_id(0) == 1)
    def _():
        out[...] = base[...] + decoded(other[...])


def added(core, base, same, other, at, partial):
    rows, width = same.shape
    unit = ADD_ROWS
    halves = base.shape[0] // 2 // unit
    whole = pl.BlockSpec((unit, width), lambda h, r, core: ((h ^ core[0]) * halves + at // unit + r, 0))
    last = rows // unit - 1
    in_specs = [
        whole,
        pl.BlockSpec((unit, width), lambda h, r, core: (r * (1 - h) + last * h, 0)),
        pl.BlockSpec((unit, width), lambda h, r, core: (r * h, 0)),
    ]
    args = [core, base, same, other]
    aliases = {}
    if partial is not None:
        in_specs.append(pl.BlockSpec(memory_space=pl.ANY))
        args.append(partial)
        aliases = {4: 0}
    return pl.pallas_call(
        add_kernel,
        grid_spec=pltpu.PrefetchScalarGridSpec(
            num_scalar_prefetch=1, grid=(2, rows // unit), in_specs=in_specs, out_specs=whole
        ),
        out_shape=jax.ShapeDtypeStruct(base.shape, base.dtype),
        input_output_aliases=aliases,
        compiler_params=pltpu.CompilerParams(vmem_limit_bytes=16 * 2**20),
        name="add",
    )(*args)


def local(task_vectors, thresholds, base_weight):
    own = task_vectors[0]
    width = own.shape[1] // 8
    x_lo, z, y, core = (lax.axis_index(name) for name in ("x_lo", "z", "y", "core"))
    place = jnp.arange(8, dtype=jnp.int32)
    to_x_hi, to_y = columns_of(place // 4, y, place % 4, core)
    order = to_x_hi * 4 + to_y
    one = core[None].astype(jnp.int32)

    def column(hops, flip):
        to_x_lo, to_z = moved(x_lo, z, core, hops, flip)
        to_x_hi, to_y = columns_of(to_x_lo, y, to_z, core)
        return to_x_hi * 4 + to_y

    def source(hops, flip):
        from_x_lo, from_z = moved(x_lo, z, core, 4 - hops, flip)
        return from_x_lo * 4 + from_z

    sources = jnp.stack([source(*step) for step in ((0, 0), *STEPS)])

    def send(block, step):
        return lax.ppermute(block, AXES, pairs(meet(*step)))

    def send_home(codes):
        return [lax.ppermute(code, AXES, pairs(home(half))) for half, code in enumerate(codes)]

    starts = [sum(CHUNKS[:i]) for i in range(len(CHUNKS))]
    tasks = lax.all_to_all(
        packed(own, order, 0, CHUNKS[0]), ("x_lo", "z"), split_axis=0, concat_axis=0, tiled=True
    )
    blocks = [
        [lax.dynamic_slice(own, (at, column(*step) * width), (rows, width)) for step in ((0, 0), *STEPS)]
        for at, rows in zip(starts[1:], CHUNKS[1:])
    ]
    codes = coded_mean(tasks, thresholds, one)
    arrived, homes = None, []
    for here, early in zip(blocks, EARLY):
        if arrived is not None:
            here[1:], arrived[GATE_ON] = lax.optimization_barrier((here[1:], arrived[GATE_ON]))
            codes = coded_mean_of(arrived, sources, thresholds, one)
        sent = [send(block, step) for block, step in zip(here[1 : 1 + early], STEPS)]
        late, codes = lax.optimization_barrier((here[1 + early :], codes))
        homes.append(send_home(codes))
        arrived = here[:1] + sent + [send(block, step) for block, step in zip(late, STEPS[early:])]
    codes = coded_mean_of(arrived, sources, thresholds, one)
    homes.append(send_home(codes))
    out = None
    for (same, other), at in zip(homes, starts):
        out = added(one, base_weight, same, other, at, out)
    return out


def solution(mesh):
    finer = Mesh(mesh.devices.reshape(tuple(SIZES.values())), AXES)
    ckpt, shard = ("x_lo", "z"), ("x_hi", "y", "core")
    return jax.shard_map(
        local,
        mesh=finer,
        in_specs=(P(ckpt, shard, None), P(), P(ckpt, shard)),
        out_specs=P(ckpt, shard),
        check_vma=False,
    )
```

time: 143 us -> 135 us (0.944)
  the two profiles are of different devices: /device:TPU:30 before, /device:TPU:27 now
where the time goes in v2:
time: 135 us
  waiting for transfers between devices  80.8 us (60%)
  starting transfers between devices  25.4 us (19%)
  Pallas kernels  20.3 us (15%)
  local copies, waits for them, and re-layouts  7.82 us (6%)
    all_to_all x1, waiting for transfers between devices, local(): lax.all_to_all(packed(own, order, 0, CHUNKS[0]), ('x_lo', 'z'), split_axi...  60.4 us
    ppermute x7, waiting for transfers between devices, send(): return lax.ppermute(block, AXES, pairs(meet(*step)))  13.8 us
    ppermute x7, starting transfers between devices, send(): return lax.ppermute(block, AXES, pairs(meet(*step)))  9.84 us
    ppermute x4, starting transfers between devices, send_home(): lax.ppermute(code, AXES, pairs(home(half)))  9.36 us
    pallas_call x1, Pallas kernels, coded_mean(): pl.pallas_call(mean_kernel, grid_spec=pltpu.PrefetchScalarGridSpec(num_sc...  7.52 us
    ppermute x4, waiting for transfers between devices, send_home(): lax.ppermute(code, AXES, pairs(home(half)))  6.56 us
    all_to_all x1, starting transfers between devices, local(): lax.all_to_all(packed(own, order, 0, CHUNKS[0]), ('x_lo', 'z'), split_axi...  6.22 us
    pallas_call x1, Pallas kernels, packed(): pl.pallas_call(functools.partial(pack_kernel, at), in_specs=[pl.BlockSpec...  6.21 us
  transfers between devices with their start and end apart: 12, of which 6 were waited for; matrix products, arithmetic and copies ran while one was open for 2% of the time, Pallas kernels for 10%

profile of v2, /device:TPU:27, one launch (start us, length us, event | category | flops | bytes accessed | tf_op | source)
XLA Modules:
  0.0 134.9 jit_solution(10510319060589207855)
XLA Ops:
  0.5 6.2 %pack.1 = bf16[8,192,2048]{2,1,0:T(8,128)(2,1)} custom-call(s32[8]{0:T(128)} %fusion.3.order, bf16[256,16384]{1,0:T(8,128)(2,1)} %bitcast.26), custom_call_target="tpu_custom_call" | custom-call | tf_op jit(solution)/shard_map/pack/pallas_call | solution.py:79
  6.8 6.2 %all-to-all-start = ((bf16[8,192,2048]{2,1,0:T(8,128)(2,1)}), bf16[8,192,2048]{2,1,0:T(8,128)(2,1)}, u32[]{:S(2)}, u32[]{:S(2)}) async-start(bf16[8,192,2048]{2,1,0:T(8,128)(2,1)} %pack.1), calls=%async_computation | async-start | bytes 12582912 | tf_op jit(solution)/shard_map/all_to_all | solution.py:255
  13.0 2.8 %dynamic-slice_bitcast_fusion = (bf16[64,2048]{1,0:T(8,128)(2,1)}, bf16[64,2048]{1,0:T(8,128)(2,1)}, bf16[64,2048]{1,0:T(8,128)(2,1)}, bf16[64,2048]{1,0:T(8,128...) fusion(bf16[1,256,16384]{2,1,0:T(8,128)(2,1)} %param.3, ...), kind=kLoop, calls=%fused_computation | loop fusion | bytes 4194336 | tf_op jit(solution)/shard_map/dynamic_slice | solution.py:259
  15.8 1.2 collective-permute-start.4
  16.9 1.3 collective-permute-start.3
  18.2 1.7 %collective-permute-start.2 = (bf16[64,2048]{1,0:T(8,128)(2,1)}, bf16[64,2048]{1,0:T(8,128)(2,1)S(1)}, u32[]{:S(2)}, u32[]{:S(2)}) collective-permute-start(bf16[64,2048]{1,0:T(8,128)(2,1)} %get-tuple-element.25), channel_id=1, source_target_pairs={{0,32},{1,33},{2,34},{3,35},{4,36},{5,37},{6,38},{7,39},{8,40},{9,... | collective-permute-start | bytes 786440 | tf_op jit(solution)/shard_map/ppermute | solution.py:249
  19.9 1.2 collective-permute-start.1
  21.2 2.3 %collective-permute-start = (bf16[64,2048]{1,0:T(8,128)(2,1)}, bf16[64,2048]{1,0:T(8,128)(2,1)}, u32[]{:S(2)}, u32[]{:S(2)}) collective-permute-start(bf16[64,2048]{1,0:T(8,128)(2,1)} %get-tuple-element.27), channel_id=1, source_target_pairs={{0,16},{1,49},{2,18},{3,51},{4,20},{5,53},{6,22},{7,55},{8,24},{9,... | collective-permute-start | bytes 786440 | tf_op jit(solution)/shard_map/ppermute | solution.py:249
  23.5 60.4 %all-to-all-done.tasks_same.tasks_other = bf16[8,192,2048]{2,1,0:T(8,128)(2,1)} async-done(((bf16[8,192,2048]{2,1,0:T(8,128)(2,1)}), bf16[8,192,2048]{2,1,0:T(8,128)(2,1)}, u32[]{:S(2)}, u32[]{:S(2)}) %all-to-all-start) | async-done | bytes 6291488 | tf_op jit(solution)/shard_map/all_to_all | solution.py:255
  83.9 7.5 %mean.1 = (bf16[192,1024]{1,0:T(8,128)(2,1)}, bf16[192,1024]{1,0:T(8,128)(2,1)}) custom-call(s32[1]{0:T(128)} %bitcast.core, f32[8]{0:T(128)S(1)} %copy-done.7, bf16[8,192,2048]{2,1,0:T(8,128)(2,1)} %all-to-all-done.tasks_same.tasks_other, bf16[8,192,2048]{2,1,0:T(8,128)(2,1)} %all-to-all-done.tasks_same.tasks_other), custom_call_target="tpu_custom_call" | custom-call | tf_op jit(solution)/shard_map/mean/pallas_call | solution.py:139
  91.4 9.3 %collective-permute-done.4.refs_5_ = bf16[64,2048]{1,0:T(8,128)(2,1)S(1)} collective-permute-done((bf16[64,2048]{1,0:T(8,128)(2,1)}, bf16[64,2048]{1,0:T(8,128)(2,1)S(1)}, u32[]{:S(2)}, u32[]{:S(2)}) %collective-permute-start.4) | collective-permute-done | bytes 262176 | tf_op jit(solution)/shard_map/ppermute | solution.py:249
  102.1 1.5 %collective-permute-start.6 = (bf16[64,2048]{1,0:T(8,128)(2,1)}, bf16[64,2048]{1,0:T(8,128)(2,1)}, u32[]{:S(2)}, u32[]{:S(2)}) collective-permute-start(bf16[64,2048]{1,0:T(8,128)(2,1)} %get-tuple-element.16), channel_id=1, source_target_pairs={{0,64},{1,65},{2,66},{3,67},{4,68},{5,69},{6,70},{7,71},{8,72},{9,... | collective-permute-start | bytes 786440 | tf_op jit(solution)/shard_map/ppermute | solution.py:249
  104.2 2.1 %collective-permute-start.9 = (bf16[192,1024]{1,0:T(8,128)(2,1)}, bf16[192,1024]{1,0:T(8,128)(2,1)S(1)}, u32[]{:S(2)}, u32[]{:S(2)}) collective-permute-start(bf16[192,1024]{1,0:T(8,128)(2,1)} %get-tuple-element.19), channel_id=1, source_target_pairs={{0,0},{1,5},{2,22},{3,19},{4,36},{5,33},{6,50},{7,55},{8,64},{9,69... | collective-permute-start | bytes 1179656 | tf_op jit(solution)/shard_map/ppermute | solution.py:252
  107.1 2.7 %collective-permute-start.10 = (bf16[192,1024]{1,0:T(8,128)(2,1)}, bf16[192,1024]{1,0:T(8,128)(2,1)S(1)}, u32[]{:S(2)}, u32[]{:S(2)}) collective-permute-start(bf16[192,1024]{1,0:T(8,128)(2,1)} %get-tuple-element.20), channel_id=1, source_target_pairs={{0,1},{1,4},{2,23},{3,18},{4,37},{5,32},{6,51},{7,54},{8,65},{9,68... | collective-permute-start | bytes 1179656 | tf_op jit(solution)/shard_map/ppermute | solution.py:252
  110.6 3.8 %collective-permute-done.6.refs_7_ = bf16[64,2048]{1,0:T(8,128)(2,1)} collective-permute-done((bf16[64,2048]{1,0:T(8,128)(2,1)}, bf16[64,2048]{1,0:T(8,128)(2,1)}, u32[]{:S(2)}, u32[]{:S(2)}) %collective-permute-start.6) | collective-permute-done | bytes 262176 | tf_op jit(solution)/shard_map/ppermute | solution.py:249
  114.4 0.9 copy-done.2
  115.4 0.9 copy-done.4
  116.3 0.9 copy-done.6
  117.3 3.1 %mean_of_blocks.1 = (bf16[64,1024]{1,0:T(8,128)(2,1)S(1)}, bf16[64,1024]{1,0:T(8,128)(2,1)S(1)}) custom-call(s32[1]{0:T(128)} %bitcast.core, s32[8]{0:T(128)S(1)} %stack.35.source, f32[8]{0:T(128)S(1)} %copy-done.7, bf16[64,2048]{1,0:T(8,128)(2,1)S(1)} %get-tuple-element.28.refs_0_, bf16[64,2048]{1,0:T(8,128)(2,1)} %collective-permute-done.refs_1_, ...), custom_call_target="tpu_custom_call" | custom-call | tf_op jit(solution)/shard_map/mean_of_blocks/pallas_call | solution.py:173
  120.4 2.0 %collective-permute-start.7 = (bf16[64,1024]{1,0:T(8,128)(2,1)S(1)}, bf16[64,1024]{1,0:T(8,128)(2,1)S(1)}, u32[]{:S(2)}, u32[]{:S(2)}) collective-permute-start(bf16[64,1024]{1,0:T(8,128)(2,1)S(1)} %get-tuple-element.17), channel_id=1, source_target_pairs={{0,0},{1,5},{2,22},{3,19},{4,36},{5,33},{6,50},{7,55},{8,64},{9,69... | collective-permute-start | bytes 393224 | tf_op jit(solution)/shard_map/ppermute | solution.py:252
  122.4 2.5 %collective-permute-start.8 = (bf16[64,1024]{1,0:T(8,128)(2,1)S(1)}, bf16[64,1024]{1,0:T(8,128)(2,1)S(1)}, u32[]{:S(2)}, u32[]{:S(2)}) collective-permute-start(bf16[64,1024]{1,0:T(8,128)(2,1)S(1)} %get-tuple-element.18), channel_id=1, source_target_pairs={{0,1},{1,4},{2,23},{3,18},{4,37},{5,32},{6,51},{7,54},{8,65},{9,68... | collective-permute-start | bytes 393224 | tf_op jit(solution)/shard_map/ppermute | solution.py:252
  124.9 4.3 %collective-permute-done.10.other = bf16[192,1024]{1,0:T(8,128)(2,1)S(1)} collective-permute-done((bf16[192,1024]{1,0:T(8,128)(2,1)}, bf16[192,1024]{1,0:T(8,128)(2,1)S(1)}, u32[]{:S(2)}, u32[]{:S(2)}) %collective-permute-start.10) | collective-permute-done | bytes 393248 | tf_op jit(solution)/shard_map/ppermute | solution.py:252
  129.2 2.5 %add.304.rest_0_ = f32[512,1024]{1,0:T(8,128)} custom-call(s32[1]{0:T(128)} %bitcast.core, f32[512,1024]{1,0:T(8,128)S(1)} %copy-done, bf16[192,1024]{1,0:T(8,128)(2,1)S(1)} %collective-permute-done.9.same, bf16[192,1024]{1,0:T(8,128)(2,1)S(1)} %collective-permute-done.10.other), custom_call_target="tpu_custom_call" | custom-call | tf_op jit(solution)/shard_map/add/pallas_call | solution.py:216
  131.8 2.2 %collective-permute-done.8.other = bf16[64,1024]{1,0:T(8,128)(2,1)S(1)} collective-permute-done((bf16[64,1024]{1,0:T(8,128)(2,1)S(1)}, bf16[64,1024]{1,0:T(8,128)(2,1)S(1)}, u32[]{:S(2)}, u32[]{:S(2)}) %collective-permute-start.8) | collective-permute-done | bytes 131104 | tf_op jit(solution)/shard_map/ppermute | solution.py:252
  (24 shorter events, 4.9 us)
Async XLA Ops:
  6.7 77.2 %copy-start.7 = (f32[8]{0:T(128)S(1)}, f32[8]{0:T(128)}, u32[]{:S(2)}) copy-start(f32[8]{0:T(128)} %thresholds.1) | copy-start | bytes 100
  6.8 77.1 %all-to-all-start = ((bf16[8,192,2048]{2,1,0:T(8,128)(2,1)}), bf16[8,192,2048]{2,1,0:T(8,128)(2,1)}, u32[]{:S(2)}, u32[]{:S(2)}) async-start(bf16[8,192,2048]{2,1,0:T(8,128)(2,1)} %pack.1), calls=%async_computation | async-start | bytes 12582912 | tf_op jit(solution)/shard_map/all_to_all | solution.py:255
  15.8 85.0 %collective-permute-start.4 = (bf16[64,2048]{1,0:T(8,128)(2,1)}, bf16[64,2048]{1,0:T(8,128)(2,1)S(1)}, u32[]{:S(2)}, u32[]{:S(2)}) collective-permute-start(bf16[64,2048]{1,0:T(8,128)(2,1)} %get-tuple-element.23), channel_id=1, source_target_pairs={{0,48},{1,17},{2,50},{3,19},{4,52},{5,21},{6,54},{7,23},{8,56},{9,... | collective-permute-start | bytes 786440 | tf_op jit(solution)/shard_map/ppermute | solution.py:249
  16.9 84.4 %collective-permute-start.3 = (bf16[64,2048]{1,0:T(8,128)(2,1)}, bf16[64,2048]{1,0:T(8,128)(2,1)S(1)}, u32[]{:S(2)}, u32[]{:S(2)}) collective-permute-start(bf16[64,2048]{1,0:T(8,128)(2,1)} %get-tuple-element.24), channel_id=1, source_target_pairs={{0,80},{1,113},{2,82},{3,115},{4,84},{5,117},{6,86},{7,119},{8,88}... | collective-permute-start | bytes 786440 | tf_op jit(solution)/shard_map/ppermute | solution.py:249
  18.2 85.3 %collective-permute-start.2 = (bf16[64,2048]{1,0:T(8,128)(2,1)}, bf16[64,2048]{1,0:T(8,128)(2,1)S(1)}, u32[]{:S(2)}, u32[]{:S(2)}) collective-permute-start(bf16[64,2048]{1,0:T(8,128)(2,1)} %get-tuple-element.25), channel_id=1, source_target_pairs={{0,32},{1,33},{2,34},{3,35},{4,36},{5,37},{6,38},{7,39},{8,40},{9,... | collective-permute-start | bytes 786440 | tf_op jit(solution)/shard_map/ppermute | solution.py:249
  19.9 86.5 %collective-permute-start.1 = (bf16[64,2048]{1,0:T(8,128)(2,1)}, bf16[64,2048]{1,0:T(8,128)(2,1)S(1)}, u32[]{:S(2)}, u32[]{:S(2)}) collective-permute-start(bf16[64,2048]{1,0:T(8,128)(2,1)} %get-tuple-element.26), channel_id=1, source_target_pairs={{0,112},{1,81},{2,114},{3,83},{4,116},{5,85},{6,118},{7,87},{8,120... | collective-permute-start | bytes 786440 | tf_op jit(solution)/shard_map/ppermute | solution.py:249
  21.2 88.8 %collective-permute-start = (bf16[64,2048]{1,0:T(8,128)(2,1)}, bf16[64,2048]{1,0:T(8,128)(2,1)}, u32[]{:S(2)}, u32[]{:S(2)}) collective-permute-start(bf16[64,2048]{1,0:T(8,128)(2,1)} %get-tuple-element.27), channel_id=1, source_target_pairs={{0,16},{1,49},{2,18},{3,51},{4,20},{5,53},{6,22},{7,55},{8,24},{9,... | collective-permute-start | bytes 786440 | tf_op jit(solution)/shard_map/ppermute | solution.py:249
  83.9 45.3 %copy-start = (f32[512,1024]{1,0:T(8,128)S(1)}, f32[512,1024]{1,0:T(8,128)}, u32[]{:S(2)}) copy-start(f32[512,1024]{1,0:T(8,128)} %base.3) | copy-start | bytes 6291460
  100.7 9.8 %collective-permute-start.5 = (bf16[64,2048]{1,0:T(8,128)(2,1)}, bf16[64,2048]{1,0:T(8,128)(2,1)}, u32[]{:S(2)}, u32[]{:S(2)}) collective-permute-start(bf16[64,2048]{1,0:T(8,128)(2,1)} %get-tuple-element.15), channel_id=1, source_target_pairs={{0,96},{1,97},{2,98},{3,99},{4,100},{5,101},{6,102},{7,103},{8,104... | collective-permute-start | bytes 786440 | tf_op jit(solution)/shard_map/ppermute | solution.py:249
  101.4 0.7 copy-start.1
  102.1 12.3 %collective-permute-start.6 = (bf16[64,2048]{1,0:T(8,128)(2,1)}, bf16[64,2048]{1,0:T(8,128)(2,1)}, u32[]{:S(2)}, u32[]{:S(2)}) collective-permute-start(bf16[64,2048]{1,0:T(8,128)(2,1)} %get-tuple-element.16), channel_id=1, source_target_pairs={{0,64},{1,65},{2,66},{3,67},{4,68},{5,69},{6,70},{7,71},{8,72},{9,... | collective-permute-start | bytes 786440 | tf_op jit(solution)/shard_map/ppermute | solution.py:249
  103.5 0.7 copy-start.3
  104.2 20.6 %collective-permute-start.9 = (bf16[192,1024]{1,0:T(8,128)(2,1)}, bf16[192,1024]{1,0:T(8,128)(2,1)S(1)}, u32[]{:S(2)}, u32[]{:S(2)}) collective-permute-start(bf16[192,1024]{1,0:T(8,128)(2,1)} %get-tuple-element.19), channel_id=1, source_target_pairs={{0,0},{1,5},{2,22},{3,19},{4,36},{5,33},{6,50},{7,55},{8,64},{9,69... | collective-permute-start | bytes 1179656 | tf_op jit(solution)/shard_map/ppermute | solution.py:252
  106.4 0.7 copy-start.5
  107.1 22.1 %collective-permute-start.10 = (bf16[192,1024]{1,0:T(8,128)(2,1)}, bf16[192,1024]{1,0:T(8,128)(2,1)S(1)}, u32[]{:S(2)}, u32[]{:S(2)}) collective-permute-start(bf16[192,1024]{1,0:T(8,128)(2,1)} %get-tuple-element.20), channel_id=1, source_target_pairs={{0,1},{1,4},{2,23},{3,18},{4,37},{5,32},{6,51},{7,54},{8,65},{9,68... | collective-permute-start | bytes 1179656 | tf_op jit(solution)/shard_map/ppermute | solution.py:252
  114.4 1.0 copy-start.2
  115.4 0.9 copy-start.4
  116.3 0.9 copy-start.6
  120.4 11.4 %collective-permute-start.7 = (bf16[64,1024]{1,0:T(8,128)(2,1)S(1)}, bf16[64,1024]{1,0:T(8,128)(2,1)S(1)}, u32[]{:S(2)}, u32[]{:S(2)}) collective-permute-start(bf16[64,1024]{1,0:T(8,128)(2,1)S(1)} %get-tuple-element.17), channel_id=1, source_target_pairs={{0,0},{1,5},{2,22},{3,19},{4,36},{5,33},{6,50},{7,55},{8,64},{9,69... | collective-permute-start | bytes 393224 | tf_op jit(solution)/shard_map/ppermute | solution.py:252
  122.4 11.6 %collective-permute-start.8 = (bf16[64,1024]{1,0:T(8,128)(2,1)S(1)}, bf16[64,1024]{1,0:T(8,128)(2,1)S(1)}, u32[]{:S(2)}, u32[]{:S(2)}) collective-permute-start(bf16[64,1024]{1,0:T(8,128)(2,1)S(1)} %get-tuple-element.18), channel_id=1, source_target_pairs={{0,1},{1,4},{2,23},{3,18},{4,37},{5,32},{6,51},{7,54},{8,65},{9,68... | collective-permute-start | bytes 393224 | tf_op jit(solution)/shard_map/ppermute | solution.py:252

commit v3 on v2

--- a/solution.py
+++ b/solution.py
@@ -9,13 +9,13 @@
 
 SIZES = dict(x_lo=2, z=4, x_hi=2, y=4, core=2)
 AXES = tuple(SIZES)
-CHUNKS = (192, 64)
+CHUNKS = (160, 96)
 STEPS = ((1, 0), (3, 1), (2, 0), (1, 1), (3, 0), (2, 1), (0, 1))
-EARLY, GATE_ON = (5,), 4
+EARLY, GATE_ON = (4,), 4
 AHEAD = 8
 LIFT = 4.0
 SCALE, SHIFT = 1920.0, -120.0
-BLOCK_ROWS, ADD_ROWS = 64, 64
+BLOCK_ROWS, BLOCK_ROWS_B, ADD_ROWS = 80, 48, (80, 96)
 TILE_ROWS, SLICE = 16, 128
 
 
@@ -168,7 +168,7 @@
 def coded_mean_of(blocks, source, thresholds, core):
     rows, width = blocks[0].shape
     out = jax.ShapeDtypeStruct((rows, width // 2), jnp.bfloat16)
-    unit = min(rows, BLOCK_ROWS)
+    unit = min(rows, BLOCK_ROWS_B)
     block = pl.BlockSpec((unit, width), lambda r, *_: (r, 0))
     return pl.pallas_call(
         blocks_kernel,
@@ -196,15 +196,18 @@
         out[...] = base[...] + decoded(other[...])
 
 
-def added(core, base, same, other, at, partial):
+def added(core, base, same, other, at, partial, unit):
     rows, width = same.shape
-    unit = ADD_ROWS
-    halves = base.shape[0] // 2 // unit
-    whole = pl.BlockSpec((unit, width), lambda h, r, core: ((h ^ core[0]) * halves + at // unit + r, 0))
-    last = rows // unit - 1
+    half_rows = base.shape[0] // 2
+    steps = rows // unit
+
+    def place(h, r, core):
+        return pl.multiple_of((h ^ core[0]) * half_rows + at + r * unit, 8), 0
+
+    whole = pl.BlockSpec((pl.Element(unit), pl.Element(width)), place)
     in_specs = [
         whole,
-        pl.BlockSpec((unit, width), lambda h, r, core: (r * (1 - h) + last * h, 0)),
+        pl.BlockSpec((unit, width), lambda h, r, core: (r * (1 - h) + (steps - 1) * h, 0)),
         pl.BlockSpec((unit, width), lambda h, r, core: (r * h, 0)),
     ]
     args = [core, base, same, other]
@@ -216,7 +219,7 @@
     return pl.pallas_call(
         add_kernel,
         grid_spec=pltpu.PrefetchScalarGridSpec(
-            num_scalar_prefetch=1, grid=(2, rows // unit), in_specs=in_specs, out_specs=whole
+            num_scalar_prefetch=1, grid=(2, steps), in_specs=in_specs, out_specs=whole
         ),
         out_shape=jax.ShapeDtypeStruct(base.shape, base.dtype),
         input_output_aliases=aliases,
@@ -272,8 +275,8 @@
     codes = coded_mean_of(arrived, sources, thresholds, one)
     homes.append(send_home(codes))
     out = None
-    for (same, other), at in zip(homes, starts):
-        out = added(one, base_weight, same, other, at, out)
+    for (same, other), at, unit in zip(homes, starts, ADD_ROWS):
+        out = added(one, base_weight, same, other, at, out, unit)
     return out
 
 

time: 135 us -> 132 us (0.978)
  local copies, waits for them, and re-layouts: 7.82 us -> 3.49 us
  waiting for transfers between devices: 80.8 us -> 78.6 us
  starting transfers between devices: 25.4 us -> 27.4 us
    all_to_all x1, waiting for transfers between devices: 60.4 us -> 50.4 us  [local(): lax.all_to_all(packed(own, order, 0, CHUNKS[0]), ('x_lo', 'z'), split_axi...]
    ppermute x7, waiting for transfers between devices: 13.8 us -> 21.8 us  [send(): return lax.ppermute(block, AXES, pairs(meet(*step)))]
    unnamed x16 -> x4, local copies, waits for them, and re-layouts: 4.95 us -> 0.01 us
    ppermute x4, starting transfers between devices: 9.36 us -> 12.2 us  [send_home(): lax.ppermute(code, AXES, pairs(home(half)))]
  transfers between devices with their start and end apart: 12 -> 12, of which waited for: 6 -> 7; matrix products, arithmetic and copies ran while one was open for 2% -> 3% of each run, Pallas kernels for 10% -> 11%
where the time goes in v3:
time: 132 us; the launch traced here: 131 us
  waiting for transfers between devices  78.6 us (60%)
  starting transfers between devices  27.4 us (21%)
  Pallas kernels  21.1 us (16%)
  local copies, waits for them, and re-layouts  3.49 us (3%)
    all_to_all x1, waiting for transfers between devices, local(): lax.all_to_all(packed(own, order, 0, CHUNKS[0]), ('x_lo', 'z'), split_axi...  50.4 us
    ppermute x7, waiting for transfers between devices, send(): return lax.ppermute(block, AXES, pairs(meet(*step)))  21.8 us
    ppermute x4, starting transfers between devices, send_home(): lax.ppermute(code, AXES, pairs(home(half)))  12.2 us
    ppermute x7, starting transfers between devices, send(): return lax.ppermute(block, AXES, pairs(meet(*step)))  8.9 us
    pallas_call x1, Pallas kernels, coded_mean(): pl.pallas_call(mean_kernel, grid_spec=pltpu.PrefetchScalarGridSpec(num_sc...  6.88 us
    ppermute x4, waiting for transfers between devices, send_home(): lax.ppermute(code, AXES, pairs(home(half)))  6.45 us
    all_to_all x1, starting transfers between devices, local(): lax.all_to_all(packed(own, order, 0, CHUNKS[0]), ('x_lo', 'z'), split_axi...  6.22 us
    pallas_call x1, Pallas kernels, packed(): pl.pallas_call(functools.partial(pack_kernel, at), in_specs=[pl.BlockSpec...  5.35 us
  transfers between devices with their start and end apart: 12, of which 7 were waited for; matrix products, arithmetic and copies ran while one was open for 3% of the time, Pallas kernels for 11%

profile of v3, /device:TPU:27, one launch (start us, length us, event | category | flops | bytes accessed | tf_op | source)
XLA Modules:
  0.0 131.2 jit_solution(531255336852252447)
XLA Ops:
  0.0 0.5 fusion.3.order
  0.5 5.4 %pack.1 = bf16[8,160,2048]{2,1,0:T(8,128)(2,1)} custom-call(s32[8]{0:T(128)} %fusion.3.order, bf16[256,16384]{1,0:T(8,128)(2,1)} %bitcast.26), custom_call_target="tpu_custom_call" | custom-call | tf_op jit(solution)/shard_map/pack/pallas_call | solution.py:79
  5.9 6.2 %all-to-all-start = ((bf16[8,160,2048]{2,1,0:T(8,128)(2,1)}), bf16[8,160,2048]{2,1,0:T(8,128)(2,1)}, u32[]{:S(2)}, u32[]{:S(2)}) async-start(bf16[8,160,2048]{2,1,0:T(8,128)(2,1)} %pack.1), calls=%async_computation | async-start | bytes 10485760 | tf_op jit(solution)/shard_map/all_to_all | solution.py:258
  12.1 3.4 %dynamic-slice_bitcast_fusion = (bf16[96,2048]{1,0:T(8,128)(2,1)}, bf16[96,2048]{1,0:T(8,128)(2,1)}, bf16[96,2048]{1,0:T(8,128)(2,1)}, bf16[96,2048]{1,0:T(8,128...) fusion(bf16[1,256,16384]{2,1,0:T(8,128)(2,1)} %param.3, ...), kind=kLoop, calls=%fused_computation | loop fusion | bytes 6291488 | tf_op jit(solution)/shard_map/dynamic_slice | solution.py:262
  15.5 2.4 %collective-permute-start.3 = (bf16[96,2048]{1,0:T(8,128)(2,1)}, bf16[96,2048]{1,0:T(8,128)(2,1)S(1)}, u32[]{:S(2)}, u32[]{:S(2)}) collective-permute-start(bf16[96,2048]{1,0:T(8,128)(2,1)} %get-tuple-element.26), channel_id=1, source_target_pairs={{0,80},{1,113},{2,82},{3,115},{4,84},{5,117},{6,86},{7,119},{8,88}... | collective-permute-start | bytes 1179656 | tf_op jit(solution)/shard_map/ppermute | solution.py:252
  17.9 0.6 collective-permute-start.2
  18.5 1.5 %collective-permute-start.1 = (bf16[96,2048]{1,0:T(8,128)(2,1)}, bf16[96,2048]{1,0:T(8,128)(2,1)}, u32[]{:S(2)}, u32[]{:S(2)}) collective-permute-start(bf16[96,2048]{1,0:T(8,128)(2,1)} %get-tuple-element.28), channel_id=1, source_target_pairs={{0,112},{1,81},{2,114},{3,83},{4,116},{5,85},{6,118},{7,87},{8,120... | collective-permute-start | bytes 1179656 | tf_op jit(solution)/shard_map/ppermute | solution.py:252
  20.0 2.1 %collective-permute-start = (bf16[96,2048]{1,0:T(8,128)(2,1)}, bf16[96,2048]{1,0:T(8,128)(2,1)}, u32[]{:S(2)}, u32[]{:S(2)}) collective-permute-start(bf16[96,2048]{1,0:T(8,128)(2,1)} %get-tuple-element.29), channel_id=1, source_target_pairs={{0,16},{1,49},{2,18},{3,51},{4,20},{5,53},{6,22},{7,55},{8,24},{9,... | collective-permute-start | bytes 1179656 | tf_op jit(solution)/shard_map/ppermute | solution.py:252
  22.1 50.4 %all-to-all-done.tasks_same.tasks_other = bf16[8,160,2048]{2,1,0:T(8,128)(2,1)} async-done(((bf16[8,160,2048]{2,1,0:T(8,128)(2,1)}), bf16[8,160,2048]{2,1,0:T(8,128)(2,1)}, u32[]{:S(2)}, u32[]{:S(2)}) %all-to-all-start) | async-done | bytes 5242912 | tf_op jit(solution)/shard_map/all_to_all | solution.py:258
  72.4 6.9 %mean.1 = (bf16[160,1024]{1,0:T(8,128)(2,1)}, bf16[160,1024]{1,0:T(8,128)(2,1)}) custom-call(s32[1]{0:T(128)} %bitcast.core, f32[8]{0:T(128)S(1)} %copy-done.1, bf16[8,160,2048]{2,1,0:T(8,128)(2,1)} %all-to-all-done.tasks_same.tasks_other, bf16[8,160,2048]{2,1,0:T(8,128)(2,1)} %all-to-all-done.tasks_same.tasks_other), custom_call_target="tpu_custom_call" | custom-call | tf_op jit(solution)/shard_map/mean/pallas_call | solution.py:139
  79.3 1.6 %collective-permute-start.4 = (bf16[96,2048]{1,0:T(8,128)(2,1)}, bf16[96,2048]{1,0:T(8,128)(2,1)}, u32[]{:S(2)}, u32[]{:S(2)}) collective-permute-start(bf16[96,2048]{1,0:T(8,128)(2,1)} %get-tuple-element.16), channel_id=1, source_target_pairs={{0,48},{1,17},{2,50},{3,19},{4,52},{5,21},{6,54},{7,23},{8,56},{9,... | collective-permute-start | bytes 1179656 | tf_op jit(solution)/shard_map/ppermute | solution.py:252
  80.9 0.8 collective-permute-start.5
  81.7 6.2 %collective-permute-done.2.refs_3_ = bf16[96,2048]{1,0:T(8,128)(2,1)S(1)} collective-permute-done((bf16[96,2048]{1,0:T(8,128)(2,1)}, bf16[96,2048]{1,0:T(8,128)(2,1)S(1)}, u32[]{:S(2)}, u32[]{:S(2)}) %collective-permute-start.2) | collective-permute-done | bytes 393248 | tf_op jit(solution)/shard_map/ppermute | solution.py:252
  88.0 4.9 %collective-permute-start.9 = (bf16[160,1024]{1,0:T(8,128)(2,1)}, bf16[160,1024]{1,0:T(8,128)(2,1)}, u32[]{:S(2)}, u32[]{:S(2)}) collective-permute-start(bf16[160,1024]{1,0:T(8,128)(2,1)} %get-tuple-element.21), channel_id=1, source_target_pairs={{0,0},{1,5},{2,22},{3,19},{4,36},{5,33},{6,50},{7,55},{8,64},{9,69... | collective-permute-start | bytes 983048 | tf_op jit(solution)/shard_map/ppermute | solution.py:255
  92.9 15.4 %collective-permute-done.refs_1_ = bf16[96,2048]{1,0:T(8,128)(2,1)} collective-permute-done((bf16[96,2048]{1,0:T(8,128)(2,1)}, bf16[96,2048]{1,0:T(8,128)(2,1)}, u32[]{:S(2)}, u32[]{:S(2)}) %collective-permute-start) | collective-permute-done | bytes 393248 | tf_op jit(solution)/shard_map/ppermute | solution.py:252
  108.4 2.6 %collective-permute-start.10 = (bf16[160,1024]{1,0:T(8,128)(2,1)}, bf16[160,1024]{1,0:T(8,128)(2,1)}, u32[]{:S(2)}, u32[]{:S(2)}) collective-permute-start(bf16[160,1024]{1,0:T(8,128)(2,1)} %get-tuple-element.22), channel_id=1, source_target_pairs={{0,1},{1,4},{2,23},{3,18},{4,37},{5,32},{6,51},{7,54},{8,65},{9,68... | collective-permute-start | bytes 983048 | tf_op jit(solution)/shard_map/ppermute | solution.py:255
  111.1 4.1 %mean_of_blocks.1 = (bf16[96,1024]{1,0:T(8,128)(2,1)S(1)}, bf16[96,1024]{1,0:T(8,128)(2,1)S(1)}) custom-call(s32[1]{0:T(128)} %bitcast.core, s32[8]{0:T(128)S(1)} %stack.35.source, f32[8]{0:T(128)S(1)} %copy-done.1, bf16[96,2048]{1,0:T(8,128)(2,1)S(1)} %get-tuple-element.30.refs_0_, bf16[96,2048]{1,0:T(8,128)(2,1)} %collective-permute-done.refs_1_, ...), custom_call_target="tpu_custom_call" | custom-call | tf_op jit(solution)/shard_map/mean_of_blocks/pallas_call | solution.py:173
  115.3 1.9 %collective-permute-start.7 = (bf16[96,1024]{1,0:T(8,128)(2,1)S(1)}, bf16[96,1024]{1,0:T(8,128)(2,1)S(1)}, u32[]{:S(2)}, u32[]{:S(2)}) collective-permute-start(bf16[96,1024]{1,0:T(8,128)(2,1)S(1)} %get-tuple-element.19), channel_id=1, source_target_pairs={{0,0},{1,5},{2,22},{3,19},{4,36},{5,33},{6,50},{7,55},{8,64},{9,69... | collective-permute-start | bytes 589832 | tf_op jit(solution)/shard_map/ppermute | solution.py:255
  117.2 2.8 %collective-permute-start.8 = (bf16[96,1024]{1,0:T(8,128)(2,1)S(1)}, bf16[96,1024]{1,0:T(8,128)(2,1)S(1)}, u32[]{:S(2)}, u32[]{:S(2)}) collective-permute-start(bf16[96,1024]{1,0:T(8,128)(2,1)S(1)} %get-tuple-element.20), channel_id=1, source_target_pairs={{0,1},{1,4},{2,23},{3,18},{4,37},{5,32},{6,51},{7,54},{8,65},{9,68... | collective-permute-start | bytes 589832 | tf_op jit(solution)/shard_map/ppermute | solution.py:255
  120.0 2.7 %collective-permute-done.10.other = bf16[160,1024]{1,0:T(8,128)(2,1)} collective-permute-done((bf16[160,1024]{1,0:T(8,128)(2,1)}, bf16[160,1024]{1,0:T(8,128)(2,1)}, u32[]{:S(2)}, u32[]{:S(2)}) %collective-permute-start.10) | collective-permute-done | bytes 327712 | tf_op jit(solution)/shard_map/ppermute | solution.py:255
  122.7 3.6 %add.304.rest_0_ = f32[512,1024]{1,0:T(8,128)} custom-call(s32[1]{0:T(128)} %bitcast.core, f32[512,1024]{1,0:T(8,128)S(1)} %copy-done, bf16[160,1024]{1,0:T(8,128)(2,1)} %collective-permute-done.9.same, bf16[160,1024]{1,0:T(8,128)(2,1)} %collective-permute-done.10.other), custom_call_target="tpu_custom_call" | custom-call | tf_op jit(solution)/shard_map/add/pallas_call | solution.py:219
  126.4 0.8 collective-permute-done.7.same
  127.1 2.9 %collective-permute-done.8.other = bf16[96,1024]{1,0:T(8,128)(2,1)S(1)} collective-permute-done((bf16[96,1024]{1,0:T(8,128)(2,1)S(1)}, bf16[96,1024]{1,0:T(8,128)(2,1)S(1)}, u32[]{:S(2)}, u32[]{:S(2)}) %collective-permute-start.8) | collective-permute-done | bytes 196640 | tf_op jit(solution)/shard_map/ppermute | solution.py:255
  130.1 1.1 add.305
  (12 shorter events, 0.3 us)
Async XLA Ops:
  5.9 66.5 %all-to-all-start = ((bf16[8,160,2048]{2,1,0:T(8,128)(2,1)}), bf16[8,160,2048]{2,1,0:T(8,128)(2,1)}, u32[]{:S(2)}, u32[]{:S(2)}) async-start(bf16[8,160,2048]{2,1,0:T(8,128)(2,1)} %pack.1), calls=%async_computation | async-start | bytes 10485760 | tf_op jit(solution)/shard_map/all_to_all | solution.py:258
  12.1 60.3 %copy-start.1 = (f32[8]{0:T(128)S(1)}, f32[8]{0:T(128)}, u32[]{:S(2)}) copy-start(f32[8]{0:T(128)} %thresholds.1) | copy-start | bytes 100
  15.5 65.3 %collective-permute-start.3 = (bf16[96,2048]{1,0:T(8,128)(2,1)}, bf16[96,2048]{1,0:T(8,128)(2,1)S(1)}, u32[]{:S(2)}, u32[]{:S(2)}) collective-permute-start(bf16[96,2048]{1,0:T(8,128)(2,1)} %get-tuple-element.26), channel_id=1, source_target_pairs={{0,80},{1,113},{2,82},{3,115},{4,84},{5,117},{6,86},{7,119},{8,88}... | collective-permute-start | bytes 1179656 | tf_op jit(solution)/shard_map/ppermute | solution.py:252
  17.9 69.9 %collective-permute-start.2 = (bf16[96,2048]{1,0:T(8,128)(2,1)}, bf16[96,2048]{1,0:T(8,128)(2,1)S(1)}, u32[]{:S(2)}, u32[]{:S(2)}) collective-permute-start(bf16[96,2048]{1,0:T(8,128)(2,1)} %get-tuple-element.27), channel_id=1, source_target_pairs={{0,32},{1,33},{2,34},{3,35},{4,36},{5,37},{6,38},{7,39},{8,40},{9,... | collective-permute-start | bytes 1179656 | tf_op jit(solution)/shard_map/ppermute | solution.py:252
  18.5 69.6 %collective-permute-start.1 = (bf16[96,2048]{1,0:T(8,128)(2,1)}, bf16[96,2048]{1,0:T(8,128)(2,1)}, u32[]{:S(2)}, u32[]{:S(2)}) collective-permute-start(bf16[96,2048]{1,0:T(8,128)(2,1)} %get-tuple-element.28), channel_id=1, source_target_pairs={{0,112},{1,81},{2,114},{3,83},{4,116},{5,85},{6,118},{7,87},{8,120... | collective-permute-start | bytes 1179656 | tf_op jit(solution)/shard_map/ppermute | solution.py:252
  20.0 88.4 %collective-permute-start = (bf16[96,2048]{1,0:T(8,128)(2,1)}, bf16[96,2048]{1,0:T(8,128)(2,1)}, u32[]{:S(2)}, u32[]{:S(2)}) collective-permute-start(bf16[96,2048]{1,0:T(8,128)(2,1)} %get-tuple-element.29), channel_id=1, source_target_pairs={{0,16},{1,49},{2,18},{3,51},{4,20},{5,53},{6,22},{7,55},{8,24},{9,... | collective-permute-start | bytes 1179656 | tf_op jit(solution)/shard_map/ppermute | solution.py:252
  72.4 50.3 %copy-start = (f32[512,1024]{1,0:T(8,128)S(1)}, f32[512,1024]{1,0:T(8,128)}, u32[]{:S(2)}) copy-start(f32[512,1024]{1,0:T(8,128)} %base.3) | copy-start | bytes 6291460
  79.3 31.8 %collective-permute-start.4 = (bf16[96,2048]{1,0:T(8,128)(2,1)}, bf16[96,2048]{1,0:T(8,128)(2,1)}, u32[]{:S(2)}, u32[]{:S(2)}) collective-permute-start(bf16[96,2048]{1,0:T(8,128)(2,1)} %get-tuple-element.16), channel_id=1, source_target_pairs={{0,48},{1,17},{2,50},{3,19},{4,52},{5,21},{6,54},{7,23},{8,56},{9,... | collective-permute-start | bytes 1179656 | tf_op jit(solution)/shard_map/ppermute | solution.py:252
  80.9 30.3 %collective-permute-start.5 = (bf16[96,2048]{1,0:T(8,128)(2,1)}, bf16[96,2048]{1,0:T(8,128)(2,1)}, u32[]{:S(2)}, u32[]{:S(2)}) collective-permute-start(bf16[96,2048]{1,0:T(8,128)(2,1)} %get-tuple-element.17), channel_id=1, source_target_pairs={{0,96},{1,97},{2,98},{3,99},{4,100},{5,101},{6,102},{7,103},{8,104... | collective-permute-start | bytes 1179656 | tf_op jit(solution)/shard_map/ppermute | solution.py:252
  87.9 23.3 %collective-permute-start.6 = (bf16[96,2048]{1,0:T(8,128)(2,1)}, bf16[96,2048]{1,0:T(8,128)(2,1)}, u32[]{:S(2)}, u32[]{:S(2)}) collective-permute-start(bf16[96,2048]{1,0:T(8,128)(2,1)} %get-tuple-element.18), channel_id=1, source_target_pairs={{0,64},{1,65},{2,66},{3,67},{4,68},{5,69},{6,70},{7,71},{8,72},{9,... | collective-permute-start | bytes 1179656 | tf_op jit(solution)/shard_map/ppermute | solution.py:252
  88.0 32.0 %collective-permute-start.9 = (bf16[160,1024]{1,0:T(8,128)(2,1)}, bf16[160,1024]{1,0:T(8,128)(2,1)}, u32[]{:S(2)}, u32[]{:S(2)}) collective-permute-start(bf16[160,1024]{1,0:T(8,128)(2,1)} %get-tuple-element.21), channel_id=1, source_target_pairs={{0,0},{1,5},{2,22},{3,19},{4,36},{5,33},{6,50},{7,55},{8,64},{9,69... | collective-permute-start | bytes 983048 | tf_op jit(solution)/shard_map/ppermute | solution.py:255
  108.4 14.4 %collective-permute-start.10 = (bf16[160,1024]{1,0:T(8,128)(2,1)}, bf16[160,1024]{1,0:T(8,128)(2,1)}, u32[]{:S(2)}, u32[]{:S(2)}) collective-permute-start(bf16[160,1024]{1,0:T(8,128)(2,1)} %get-tuple-element.22), channel_id=1, source_target_pairs={{0,1},{1,4},{2,23},{3,18},{4,37},{5,32},{6,51},{7,54},{8,65},{9,68... | collective-permute-start | bytes 983048 | tf_op jit(solution)/shard_map/ppermute | solution.py:255
  115.3 11.8 %collective-permute-start.7 = (bf16[96,1024]{1,0:T(8,128)(2,1)S(1)}, bf16[96,1024]{1,0:T(8,128)(2,1)S(1)}, u32[]{:S(2)}, u32[]{:S(2)}) collective-permute-start(bf16[96,1024]{1,0:T(8,128)(2,1)S(1)} %get-tuple-element.19), channel_id=1, source_target_pairs={{0,0},{1,5},{2,22},{3,19},{4,36},{5,33},{6,50},{7,55},{8,64},{9,69... | collective-permute-start | bytes 589832 | tf_op jit(solution)/shard_map/ppermute | solution.py:255
  117.2 12.9 %collective-permute-start.8 = (bf16[96,1024]{1,0:T(8,128)(2,1)S(1)}, bf16[96,1024]{1,0:T(8,128)(2,1)S(1)}, u32[]{:S(2)}, u32[]{:S(2)}) collective-permute-start(bf16[96,1024]{1,0:T(8,128)(2,1)S(1)} %get-tuple-element.20), channel_id=1, source_target_pairs={{0,1},{1,4},{2,23},{3,18},{4,37},{5,32},{6,51},{7,54},{8,65},{9,68... | collective-permute-start | bytes 589832 | tf_op jit(solution)/shard_map/ppermute | solution.py:255

commit v4 on v3

--- a/solution.py
+++ b/solution.py
@@ -15,8 +15,8 @@
 AHEAD = 8
 LIFT = 4.0
 SCALE, SHIFT = 1920.0, -120.0
-BLOCK_ROWS, BLOCK_ROWS_B, ADD_ROWS = 80, 48, (80, 96)
-TILE_ROWS, SLICE = 16, 128
+BLOCK_ROWS, BLOCK_ROWS_B, ADD_ROWS = 40, 48, (160, 96)
+TILE_ROWS, SLICE = 8, 128
 
 
 def columns_of(x_lo, y, z, core):
@@ -55,11 +55,13 @@
     return [(number(place), number(target(*place))) for place in places]
 
 
-def pack_kernel(at, order, own, out, held, came, went):
+def pack_kernel(at, own, out, held, came, went):
     count, rows, width = out.shape
+    y, core = lax.axis_index("y"), lax.axis_index("core")
     loads, stores = [], []
     for i in range(count):
-        column = pl.multiple_of(order[i] * width, width)
+        to_x_hi, to_y = columns_of(i // 4, y, i % 4, core)
+        column = pl.multiple_of((to_x_hi * 4 + to_y) * width, width)
         loads.append(pltpu.make_async_copy(own.at[pl.ds(at, rows), pl.ds(column, width)], held.at[i], came.at[i]))
         stores.append(pltpu.make_async_copy(held.at[i], out.at[i], went.at[i]))
     for load in loads[:AHEAD]:
@@ -73,12 +75,12 @@
         store.wait()
 
 
-def packed(own, order, at, rows):
-    count = order.shape[0]
+def packed(own, at, rows):
+    count = SIZES["x_lo"] * SIZES["z"]
     shape = (count, rows, own.shape[1] // count)
     return pl.pallas_call(
         functools.partial(pack_kernel, at),
-        in_specs=[pl.BlockSpec(memory_space=pltpu.SMEM), pl.BlockSpec(memory_space=pl.ANY)],
+        in_specs=[pl.BlockSpec(memory_space=pl.ANY)],
         out_specs=pl.BlockSpec(memory_space=pl.ANY),
         scratch_shapes=[
             pltpu.VMEM(shape, own.dtype),
@@ -88,7 +90,7 @@
         out_shape=jax.ShapeDtypeStruct(shape, own.dtype),
         compiler_params=pltpu.CompilerParams(vmem_limit_bytes=60 * 2**20),
         name="pack",
-    )(order, own)
+    )(own)
 
 
 def coded(mean):
@@ -232,9 +234,6 @@
     own = task_vectors[0]
     width = own.shape[1] // 8
     x_lo, z, y, core = (lax.axis_index(name) for name in ("x_lo", "z", "y", "core"))
-    place = jnp.arange(8, dtype=jnp.int32)
-    to_x_hi, to_y = columns_of(place // 4, y, place % 4, core)
-    order = to_x_hi * 4 + to_y
     one = core[None].astype(jnp.int32)
 
     def column(hops, flip):
@@ -256,7 +255,7 @@
 
     starts = [sum(CHUNKS[:i]) for i in range(len(CHUNKS))]
     tasks = lax.all_to_all(
-        packed(own, order, 0, CHUNKS[0]), ("x_lo", "z"), split_axis=0, concat_axis=0, tiled=True
+        packed(own, 0, CHUNKS[0]), ("x_lo", "z"), split_axis=0, concat_axis=0, tiled=True
     )
     blocks = [
         [lax.dynamic_slice(own, (at, column(*step) * width), (rows, width)) for step in ((0, 0), *STEPS)]

time: 132 us -> 130 us (0.985)
  Pallas kernels: 21.1 us -> 19.3 us
  transfers between devices with their start and end apart: 12 -> 12, of which waited for: 7 -> 7; matrix products, arithmetic and copies ran while one was open for 3% -> 3% of each run, Pallas kernels for 11% -> 10%
where the time goes in v4:
time: 130 us
  waiting for transfers between devices  79.8 us (61%)
  starting transfers between devices  27.4 us (21%)
  Pallas kernels  19.3 us (15%)
  local copies, waits for them, and re-layouts  3.49 us (3%)
    all_to_all x1, waiting for transfers between devices, local(): lax.all_to_all(packed(own, 0, CHUNKS[0]), ('x_lo', 'z'), split_axis=0, co...  50.4 us
    ppermute x7, waiting for transfers between devices, send(): return lax.ppermute(block, AXES, pairs(meet(*step)))  21.8 us
    ppermute x4, starting transfers between devices, send_home(): lax.ppermute(code, AXES, pairs(home(half)))  12.3 us
    ppermute x7, starting transfers between devices, send(): return lax.ppermute(block, AXES, pairs(meet(*step)))  8.83 us
    ppermute x4, waiting for transfers between devices, send_home(): lax.ppermute(code, AXES, pairs(home(half)))  7.61 us
    pallas_call x1, Pallas kernels, coded_mean(): pl.pallas_call(mean_kernel, grid_spec=pltpu.PrefetchScalarGridSpec(num_sc...  6.94 us
    all_to_all x1, starting transfers between devices, local(): lax.all_to_all(packed(own, 0, CHUNKS[0]), ('x_lo', 'z'), split_axis=0, co...  6.22 us
    pallas_call x1, Pallas kernels, packed(): pl.pallas_call(functools.partial(pack_kernel, at), in_specs=[pl.BlockSpec...  4.68 us
  transfers between devices with their start and end apart: 12, of which 7 were waited for; matrix products, arithmetic and copies ran while one was open for 3% of the time, Pallas kernels for 10%

profile of v4, /device:TPU:27, one launch (start us, length us, event | category | flops | bytes accessed | tf_op | source)
XLA Modules:
  0.0 130.0 jit_solution(13483560179084856314)
XLA Ops:
  0.0 4.7 %pack.1 = bf16[8,160,2048]{2,1,0:T(8,128)(2,1)} custom-call(bf16[256,16384]{1,0:T(8,128)(2,1)} %bitcast.26), custom_call_target="tpu_custom_call" | custom-call | tf_op jit(solution)/shard_map/pack/pallas_call | solution.py:81
  4.7 6.2 %all-to-all-start = ((bf16[8,160,2048]{2,1,0:T(8,128)(2,1)}), bf16[8,160,2048]{2,1,0:T(8,128)(2,1)}, u32[]{:S(2)}, u32[]{:S(2)}) async-start(bf16[8,160,2048]{2,1,0:T(8,128)(2,1)} %pack.1), calls=%async_computation | async-start | bytes 10485760 | tf_op jit(solution)/shard_map/all_to_all | solution.py:257
  10.9 3.4 %dynamic-slice_bitcast_fusion = (bf16[96,2048]{1,0:T(8,128)(2,1)}, bf16[96,2048]{1,0:T(8,128)(2,1)}, bf16[96,2048]{1,0:T(8,128)(2,1)}, bf16[96,2048]{1,0:T(8,128...) fusion(bf16[1,256,16384]{2,1,0:T(8,128)(2,1)} %param.3, ...), kind=kLoop, calls=%fused_computation | loop fusion | bytes 6291488 | tf_op jit(solution)/shard_map/dynamic_slice | solution.py:261
  14.3 2.4 %collective-permute-start.3 = (bf16[96,2048]{1,0:T(8,128)(2,1)}, bf16[96,2048]{1,0:T(8,128)(2,1)S(1)}, u32[]{:S(2)}, u32[]{:S(2)}) collective-permute-start(bf16[96,2048]{1,0:T(8,128)(2,1)} %get-tuple-element.26), channel_id=1, source_target_pairs={{0,80},{1,113},{2,82},{3,115},{4,84},{5,117},{6,86},{7,119},{8,88}... | collective-permute-start | bytes 1179656 | tf_op jit(solution)/shard_map/ppermute | solution.py:251
  16.7 0.6 collective-permute-start.2
  17.3 1.5 %collective-permute-start.1 = (bf16[96,2048]{1,0:T(8,128)(2,1)}, bf16[96,2048]{1,0:T(8,128)(2,1)}, u32[]{:S(2)}, u32[]{:S(2)}) collective-permute-start(bf16[96,2048]{1,0:T(8,128)(2,1)} %get-tuple-element.28), channel_id=1, source_target_pairs={{0,112},{1,81},{2,114},{3,83},{4,116},{5,85},{6,118},{7,87},{8,120... | collective-permute-start | bytes 1179656 | tf_op jit(solution)/shard_map/ppermute | solution.py:251
  18.8 2.1 %collective-permute-start = (bf16[96,2048]{1,0:T(8,128)(2,1)}, bf16[96,2048]{1,0:T(8,128)(2,1)}, u32[]{:S(2)}, u32[]{:S(2)}) collective-permute-start(bf16[96,2048]{1,0:T(8,128)(2,1)} %get-tuple-element.29), channel_id=1, source_target_pairs={{0,16},{1,49},{2,18},{3,51},{4,20},{5,53},{6,22},{7,55},{8,24},{9,... | collective-permute-start | bytes 1179656 | tf_op jit(solution)/shard_map/ppermute | solution.py:251
  20.9 50.4 %all-to-all-done.tasks_same.tasks_other = bf16[8,160,2048]{2,1,0:T(8,128)(2,1)} async-done(((bf16[8,160,2048]{2,1,0:T(8,128)(2,1)}), bf16[8,160,2048]{2,1,0:T(8,128)(2,1)}, u32[]{:S(2)}, u32[]{:S(2)}) %all-to-all-start) | async-done | bytes 5242912 | tf_op jit(solution)/shard_map/all_to_all | solution.py:257
  71.2 6.9 %mean.1 = (bf16[160,1024]{1,0:T(8,128)(2,1)}, bf16[160,1024]{1,0:T(8,128)(2,1)}) custom-call(s32[1]{0:T(128)} %bitcast.core, f32[8]{0:T(128)S(1)} %copy-done.1, bf16[8,160,2048]{2,1,0:T(8,128)(2,1)} %all-to-all-done.tasks_same.tasks_other, bf16[8,160,2048]{2,1,0:T(8,128)(2,1)} %all-to-all-done.tasks_same.tasks_other), custom_call_target="tpu_custom_call" | custom-call | tf_op jit(solution)/shard_map/mean/pallas_call | solution.py:141
  78.2 1.6 %collective-permute-start.4 = (bf16[96,2048]{1,0:T(8,128)(2,1)}, bf16[96,2048]{1,0:T(8,128)(2,1)}, u32[]{:S(2)}, u32[]{:S(2)}) collective-permute-start(bf16[96,2048]{1,0:T(8,128)(2,1)} %get-tuple-element.16), channel_id=1, source_target_pairs={{0,48},{1,17},{2,50},{3,19},{4,52},{5,21},{6,54},{7,23},{8,56},{9,... | collective-permute-start | bytes 1179656 | tf_op jit(solution)/shard_map/ppermute | solution.py:251
  79.7 0.7 collective-permute-start.5
  80.5 6.2 %collective-permute-done.2.refs_3_ = bf16[96,2048]{1,0:T(8,128)(2,1)S(1)} collective-permute-done((bf16[96,2048]{1,0:T(8,128)(2,1)}, bf16[96,2048]{1,0:T(8,128)(2,1)S(1)}, u32[]{:S(2)}, u32[]{:S(2)}) %collective-permute-start.2) | collective-permute-done | bytes 393248 | tf_op jit(solution)/shard_map/ppermute | solution.py:251
  86.7 0.2 collective-permute-done.1.refs_2_
  86.8 4.9 %collective-permute-start.9 = (bf16[160,1024]{1,0:T(8,128)(2,1)}, bf16[160,1024]{1,0:T(8,128)(2,1)}, u32[]{:S(2)}, u32[]{:S(2)}) collective-permute-start(bf16[160,1024]{1,0:T(8,128)(2,1)} %get-tuple-element.21), channel_id=1, source_target_pairs={{0,0},{1,5},{2,22},{3,19},{4,36},{5,33},{6,50},{7,55},{8,64},{9,69... | collective-permute-start | bytes 983048 | tf_op jit(solution)/shard_map/ppermute | solution.py:254
  91.8 15.4 %collective-permute-done.refs_1_ = bf16[96,2048]{1,0:T(8,128)(2,1)} collective-permute-done((bf16[96,2048]{1,0:T(8,128)(2,1)}, bf16[96,2048]{1,0:T(8,128)(2,1)}, u32[]{:S(2)}, u32[]{:S(2)}) %collective-permute-start) | collective-permute-done | bytes 393248 | tf_op jit(solution)/shard_map/ppermute | solution.py:251
  107.2 2.6 %collective-permute-start.10 = (bf16[160,1024]{1,0:T(8,128)(2,1)}, bf16[160,1024]{1,0:T(8,128)(2,1)}, u32[]{:S(2)}, u32[]{:S(2)}) collective-permute-start(bf16[160,1024]{1,0:T(8,128)(2,1)} %get-tuple-element.22), channel_id=1, source_target_pairs={{0,1},{1,4},{2,23},{3,18},{4,37},{5,32},{6,51},{7,54},{8,65},{9,68... | collective-permute-start | bytes 983048 | tf_op jit(solution)/shard_map/ppermute | solution.py:254
  109.9 4.1 %mean_of_blocks.1 = (bf16[96,1024]{1,0:T(8,128)(2,1)S(1)}, bf16[96,1024]{1,0:T(8,128)(2,1)S(1)}) custom-call(s32[1]{0:T(128)} %bitcast.core, s32[8]{0:T(128)S(1)} %stack.35.source, f32[8]{0:T(128)S(1)} %copy-done.1, bf16[96,2048]{1,0:T(8,128)(2,1)S(1)} %get-tuple-element.30.refs_0_, bf16[96,2048]{1,0:T(8,128)(2,1)} %collective-permute-done.refs_1_, ...), custom_call_target="tpu_custom_call" | custom-call | tf_op jit(solution)/shard_map/mean_of_blocks/pallas_call | solution.py:175
  114.1 1.9 %collective-permute-start.7 = (bf16[96,1024]{1,0:T(8,128)(2,1)S(1)}, bf16[96,1024]{1,0:T(8,128)(2,1)S(1)}, u32[]{:S(2)}, u32[]{:S(2)}) collective-permute-start(bf16[96,1024]{1,0:T(8,128)(2,1)S(1)} %get-tuple-element.19), channel_id=1, source_target_pairs={{0,0},{1,5},{2,22},{3,19},{4,36},{5,33},{6,50},{7,55},{8,64},{9,69... | collective-permute-start | bytes 589832 | tf_op jit(solution)/shard_map/ppermute | solution.py:254
  116.0 2.8 %collective-permute-start.8 = (bf16[96,1024]{1,0:T(8,128)(2,1)S(1)}, bf16[96,1024]{1,0:T(8,128)(2,1)S(1)}, u32[]{:S(2)}, u32[]{:S(2)}) collective-permute-start(bf16[96,1024]{1,0:T(8,128)(2,1)S(1)} %get-tuple-element.20), channel_id=1, source_target_pairs={{0,1},{1,4},{2,23},{3,18},{4,37},{5,32},{6,51},{7,54},{8,65},{9,68... | collective-permute-start | bytes 589832 | tf_op jit(solution)/shard_map/ppermute | solution.py:254
  118.8 2.7 %collective-permute-done.10.other = bf16[160,1024]{1,0:T(8,128)(2,1)} collective-permute-done((bf16[160,1024]{1,0:T(8,128)(2,1)}, bf16[160,1024]{1,0:T(8,128)(2,1)}, u32[]{:S(2)}, u32[]{:S(2)}) %collective-permute-start.10) | collective-permute-done | bytes 327712 | tf_op jit(solution)/shard_map/ppermute | solution.py:254
  121.5 2.4 %add.247.rest_0_ = f32[512,1024]{1,0:T(8,128)} custom-call(s32[1]{0:T(128)} %bitcast.core, f32[512,1024]{1,0:T(8,128)S(1)} %copy-done, bf16[160,1024]{1,0:T(8,128)(2,1)} %collective-permute-done.9.same, bf16[160,1024]{1,0:T(8,128)(2,1)} %collective-permute-done.10.other), custom_call_target="tpu_custom_call" | custom-call | tf_op jit(solution)/shard_map/add/pallas_call | solution.py:221
  124.0 2.0 %collective-permute-done.7.same = bf16[96,1024]{1,0:T(8,128)(2,1)S(1)} collective-permute-done((bf16[96,1024]{1,0:T(8,128)(2,1)S(1)}, bf16[96,1024]{1,0:T(8,128)(2,1)S(1)}, u32[]{:S(2)}, u32[]{:S(2)}) %collective-permute-start.7) | collective-permute-done | bytes 196640 | tf_op jit(solution)/shard_map/ppermute | solution.py:254
  125.9 2.9 %collective-permute-done.8.other = bf16[96,1024]{1,0:T(8,128)(2,1)S(1)} collective-permute-done((bf16[96,1024]{1,0:T(8,128)(2,1)S(1)}, bf16[96,1024]{1,0:T(8,128)(2,1)S(1)}, u32[]{:S(2)}, u32[]{:S(2)}) %collective-permute-start.8) | collective-permute-done | bytes 196640 | tf_op jit(solution)/shard_map/ppermute | solution.py:254
  128.9 1.1 add.248
  (11 shorter events, 0.1 us)
Async XLA Ops:
  4.7 66.5 %all-to-all-start = ((bf16[8,160,2048]{2,1,0:T(8,128)(2,1)}), bf16[8,160,2048]{2,1,0:T(8,128)(2,1)}, u32[]{:S(2)}, u32[]{:S(2)}) async-start(bf16[8,160,2048]{2,1,0:T(8,128)(2,1)} %pack.1), calls=%async_computation | async-start | bytes 10485760 | tf_op jit(solution)/shard_map/all_to_all | solution.py:257
  10.9 60.3 %copy-start.1 = (f32[8]{0:T(128)S(1)}, f32[8]{0:T(128)}, u32[]{:S(2)}) copy-start(f32[8]{0:T(128)} %thresholds.1) | copy-start | bytes 100
  14.3 65.4 %collective-permute-start.3 = (bf16[96,2048]{1,0:T(8,128)(2,1)}, bf16[96,2048]{1,0:T(8,128)(2,1)S(1)}, u32[]{:S(2)}, u32[]{:S(2)}) collective-permute-start(bf16[96,2048]{1,0:T(8,128)(2,1)} %get-tuple-element.26), channel_id=1, source_target_pairs={{0,80},{1,113},{2,82},{3,115},{4,84},{5,117},{6,86},{7,119},{8,88}... | collective-permute-start | bytes 1179656 | tf_op jit(solution)/shard_map/ppermute | solution.py:251
  16.7 69.9 %collective-permute-start.2 = (bf16[96,2048]{1,0:T(8,128)(2,1)}, bf16[96,2048]{1,0:T(8,128)(2,1)S(1)}, u32[]{:S(2)}, u32[]{:S(2)}) collective-permute-start(bf16[96,2048]{1,0:T(8,128)(2,1)} %get-tuple-element.27), channel_id=1, source_target_pairs={{0,32},{1,33},{2,34},{3,35},{4,36},{5,37},{6,38},{7,39},{8,40},{9,... | collective-permute-start | bytes 1179656 | tf_op jit(solution)/shard_map/ppermute | solution.py:251
  17.3 69.6 %collective-permute-start.1 = (bf16[96,2048]{1,0:T(8,128)(2,1)}, bf16[96,2048]{1,0:T(8,128)(2,1)}, u32[]{:S(2)}, u32[]{:S(2)}) collective-permute-start(bf16[96,2048]{1,0:T(8,128)(2,1)} %get-tuple-element.28), channel_id=1, source_target_pairs={{0,112},{1,81},{2,114},{3,83},{4,116},{5,85},{6,118},{7,87},{8,120... | collective-permute-start | bytes 1179656 | tf_op jit(solution)/shard_map/ppermute | solution.py:251
  18.8 88.4 %collective-permute-start = (bf16[96,2048]{1,0:T(8,128)(2,1)}, bf16[96,2048]{1,0:T(8,128)(2,1)}, u32[]{:S(2)}, u32[]{:S(2)}) collective-permute-start(bf16[96,2048]{1,0:T(8,128)(2,1)} %get-tuple-element.29), channel_id=1, source_target_pairs={{0,16},{1,49},{2,18},{3,51},{4,20},{5,53},{6,22},{7,55},{8,24},{9,... | collective-permute-start | bytes 1179656 | tf_op jit(solution)/shard_map/ppermute | solution.py:251
  71.2 50.3 %copy-start = (f32[512,1024]{1,0:T(8,128)S(1)}, f32[512,1024]{1,0:T(8,128)}, u32[]{:S(2)}) copy-start(f32[512,1024]{1,0:T(8,128)} %base.3) | copy-start | bytes 6291460
  78.2 31.8 %collective-permute-start.4 = (bf16[96,2048]{1,0:T(8,128)(2,1)}, bf16[96,2048]{1,0:T(8,128)(2,1)}, u32[]{:S(2)}, u32[]{:S(2)}) collective-permute-start(bf16[96,2048]{1,0:T(8,128)(2,1)} %get-tuple-element.16), channel_id=1, source_target_pairs={{0,48},{1,17},{2,50},{3,19},{4,52},{5,21},{6,54},{7,23},{8,56},{9,... | collective-permute-start | bytes 1179656 | tf_op jit(solution)/shard_map/ppermute | solution.py:251
  79.7 30.2 %collective-permute-start.5 = (bf16[96,2048]{1,0:T(8,128)(2,1)}, bf16[96,2048]{1,0:T(8,128)(2,1)}, u32[]{:S(2)}, u32[]{:S(2)}) collective-permute-start(bf16[96,2048]{1,0:T(8,128)(2,1)} %get-tuple-element.17), channel_id=1, source_target_pairs={{0,96},{1,97},{2,98},{3,99},{4,100},{5,101},{6,102},{7,103},{8,104... | collective-permute-start | bytes 1179656 | tf_op jit(solution)/shard_map/ppermute | solution.py:251
  86.7 23.3 %collective-permute-start.6 = (bf16[96,2048]{1,0:T(8,128)(2,1)}, bf16[96,2048]{1,0:T(8,128)(2,1)}, u32[]{:S(2)}, u32[]{:S(2)}) collective-permute-start(bf16[96,2048]{1,0:T(8,128)(2,1)} %get-tuple-element.18), channel_id=1, source_target_pairs={{0,64},{1,65},{2,66},{3,67},{4,68},{5,69},{6,70},{7,71},{8,72},{9,... | collective-permute-start | bytes 1179656 | tf_op jit(solution)/shard_map/ppermute | solution.py:251
  86.8 32.0 %collective-permute-start.9 = (bf16[160,1024]{1,0:T(8,128)(2,1)}, bf16[160,1024]{1,0:T(8,128)(2,1)}, u32[]{:S(2)}, u32[]{:S(2)}) collective-permute-start(bf16[160,1024]{1,0:T(8,128)(2,1)} %get-tuple-element.21), channel_id=1, source_target_pairs={{0,0},{1,5},{2,22},{3,19},{4,36},{5,33},{6,50},{7,55},{8,64},{9,69... | collective-permute-start | bytes 983048 | tf_op jit(solution)/shard_map/ppermute | solution.py:254
  107.2 14.4 %collective-permute-start.10 = (bf16[160,1024]{1,0:T(8,128)(2,1)}, bf16[160,1024]{1,0:T(8,128)(2,1)}, u32[]{:S(2)}, u32[]{:S(2)}) collective-permute-start(bf16[160,1024]{1,0:T(8,128)(2,1)} %get-tuple-element.22), channel_id=1, source_target_pairs={{0,1},{1,4},{2,23},{3,18},{4,37},{5,32},{6,51},{7,54},{8,65},{9,68... | collective-permute-start | bytes 983048 | tf_op jit(solution)/shard_map/ppermute | solution.py:254
  114.1 11.8 %collective-permute-start.7 = (bf16[96,1024]{1,0:T(8,128)(2,1)S(1)}, bf16[96,1024]{1,0:T(8,128)(2,1)S(1)}, u32[]{:S(2)}, u32[]{:S(2)}) collective-permute-start(bf16[96,1024]{1,0:T(8,128)(2,1)S(1)} %get-tuple-element.19), channel_id=1, source_target_pairs={{0,0},{1,5},{2,22},{3,19},{4,36},{5,33},{6,50},{7,55},{8,64},{9,69... | collective-permute-start | bytes 589832 | tf_op jit(solution)/shard_map/ppermute | solution.py:254
  116.0 12.9 %collective-permute-start.8 = (bf16[96,1024]{1,0:T(8,128)(2,1)S(1)}, bf16[96,1024]{1,0:T(8,128)(2,1)S(1)}, u32[]{:S(2)}, u32[]{:S(2)}) collective-permute-start(bf16[96,1024]{1,0:T(8,128)(2,1)S(1)} %get-tuple-element.20), channel_id=1, source_target_pairs={{0,1},{1,4},{2,23},{3,18},{4,37},{5,32},{6,51},{7,54},{8,65},{9,68... | collective-permute-start | bytes 589832 | tf_op jit(solution)/shard_map/ppermute | solution.py:254

commit v5 on v4

--- a/solution.py
+++ b/solution.py
@@ -155,19 +155,23 @@
     )(core, limits, tasks, tasks)
 
 
-def blocks_kernel(core, source, thresholds, *refs):
+def blocks_kernel(thresholds, *refs):
     blocks, outs = refs[:8], refs[8:]
+    x_lo, z, core = (lax.axis_index(name) for name in ("x_lo", "z", "core"))
     width = outs[0].shape[1]
-    limits = [thresholds[source[i]] for i in range(8)]
+    limits = []
+    for hops, flip in ((0, 0), *STEPS):
+        from_x_lo, from_z = moved(x_lo, z, core, 4 - hops, flip)
+        limits.append(thresholds[from_x_lo * 4 + from_z])
     for half, out in enumerate(outs):
         for row in range(0, out.shape[0], TILE_ROWS):
             for first in range(0, width, SLICE):
-                at = pl.multiple_of((core[0] ^ half) * width + first, SLICE)
+                at = pl.multiple_of((core ^ half) * width + first, SLICE)
                 values = [block[pl.ds(row, TILE_ROWS), pl.ds(at, SLICE)].astype(jnp.float32) for block in blocks]
                 out[pl.ds(row, TILE_ROWS), pl.ds(first, SLICE)] = coded(merged_tile(values, limits))
 
 
-def coded_mean_of(blocks, source, thresholds, core):
+def coded_mean_of(blocks, thresholds):
     rows, width = blocks[0].shape
     out = jax.ShapeDtypeStruct((rows, width // 2), jnp.bfloat16)
     unit = min(rows, BLOCK_ROWS_B)
@@ -175,7 +179,7 @@
     return pl.pallas_call(
         blocks_kernel,
         grid_spec=pltpu.PrefetchScalarGridSpec(
-            num_scalar_prefetch=3,
+            num_scalar_prefetch=1,
             grid=(rows // unit,),
             in_specs=[block] * 8,
             out_specs=[pl.BlockSpec((unit, width // 2), lambda r, *_: (r, 0))] * 2,
@@ -183,7 +187,7 @@
         out_shape=[out, out],
         compiler_params=pltpu.CompilerParams(vmem_limit_bytes=16 * 2**20),
         name="mean_of_blocks",
-    )(core, source, thresholds, *blocks)
+    )(thresholds, *blocks)
 
 
 def add_kernel(core, base, same, other, *rest):
@@ -240,12 +244,6 @@
         to_x_lo, to_z = moved(x_lo, z, core, hops, flip)
         to_x_hi, to_y = columns_of(to_x_lo, y, to_z, core)
         return to_x_hi * 4 + to_y
-
-    def source(hops, flip):
-        from_x_lo, from_z = moved(x_lo, z, core, 4 - hops, flip)
-        return from_x_lo * 4 + from_z
-
-    sources = jnp.stack([source(*step) for step in ((0, 0), *STEPS)])
 
     def send(block, step):
         return lax.ppermute(block, AXES, pairs(meet(*step)))
@@ -266,12 +264,12 @@
     for here, early in zip(blocks, EARLY):
         if arrived is not None:
             here[1:], arrived[GATE_ON] = lax.optimization_barrier((here[1:], arrived[GATE_ON]))
-            codes = coded_mean_of(arrived, sources, thresholds, one)
+            codes = coded_mean_of(arrived, thresholds)
         sent = [send(block, step) for block, step in zip(here[1 : 1 + early], STEPS)]
         late, codes = lax.optimization_barrier((here[1 + early :], codes))
         homes.append(send_home(codes))
         arrived = here[:1] + sent + [send(block, step) for block, step in zip(late, STEPS[early:])]
-    codes = coded_mean_of(arrived, sources, thresholds, one)
+    codes = coded_mean_of(arrived, thresholds)
     homes.append(send_home(codes))
     out = None
     for (same, other), at, unit in zip(homes, starts, ADD_ROWS):

time: 130 us -> 130 us (level)
  Pallas kernels: 19.3 us -> 16.3 us
  waiting for transfers between devices: 79.8 us -> 82.4 us
    ppermute x4, waiting for transfers between devices: 7.61 us -> 9.8 us  [send_home(): lax.ppermute(code, AXES, pairs(home(half)))]
  transfers between devices with their start and end apart: 12 -> 12, of which waited for: 7 -> 7; matrix products, arithmetic and copies ran while one was open for 3% -> 2% of each run, Pallas kernels for 10% -> 8%
where the time goes in v5:
time: 130 us
  waiting for transfers between devices  82.4 us (63%)
  starting transfers between devices  28 us (22%)
  Pallas kernels  16.3 us (13%)
  local copies, waits for them, and re-layouts  2.99 us (2%)
    all_to_all x1, waiting for transfers between devices, local(): lax.all_to_all(packed(own, 0, CHUNKS[0]), ('x_lo', 'z'), split_axis=0, co...  50.8 us
    ppermute x7, waiting for transfers between devices, send(): return lax.ppermute(block, AXES, pairs(meet(*step)))  21.8 us
    ppermute x4, starting transfers between devices, send_home(): lax.ppermute(code, AXES, pairs(home(half)))  12.2 us
    ppermute x4, waiting for transfers between devices, send_home(): lax.ppermute(code, AXES, pairs(home(half)))  9.8 us
    ppermute x7, starting transfers between devices, send(): return lax.ppermute(block, AXES, pairs(meet(*step)))  9.52 us
    pallas_call x1, Pallas kernels, coded_mean(): pl.pallas_call(mean_kernel, grid_spec=pltpu.PrefetchScalarGridSpec(num_sc...  6.25 us
    all_to_all x1, starting transfers between devices, local(): lax.all_to_all(packed(own, 0, CHUNKS[0]), ('x_lo', 'z'), split_axis=0, co...  6.22 us
    pallas_call x1, Pallas kernels, packed(): pl.pallas_call(functools.partial(pack_kernel, at), in_specs=[pl.BlockSpec...  4.68 us
  transfers between devices with their start and end apart: 12, of which 7 were waited for; matrix products, arithmetic and copies ran while one was open for 2% of the time, Pallas kernels for 8%

profile of v5, /device:TPU:27, one launch (start us, length us, event | category | flops | bytes accessed | tf_op | source)
XLA Modules:
  0.0 129.7 jit_solution(7824811251201937845)
XLA Ops:
  0.0 4.7 %pack.1 = bf16[8,160,2048]{2,1,0:T(8,128)(2,1)} custom-call(bf16[256,16384]{1,0:T(8,128)(2,1)} %bitcast.18), custom_call_target="tpu_custom_call" | custom-call | tf_op jit(solution)/shard_map/pack/pallas_call | solution.py:81
  4.7 6.2 %all-to-all-start = ((bf16[8,160,2048]{2,1,0:T(8,128)(2,1)}), bf16[8,160,2048]{2,1,0:T(8,128)(2,1)}, u32[]{:S(2)}, u32[]{:S(2)}) async-start(bf16[8,160,2048]{2,1,0:T(8,128)(2,1)} %pack.1), calls=%async_computation | async-start | bytes 10485760 | tf_op jit(solution)/shard_map/all_to_all | solution.py:255
  10.9 3.0 %dynamic-slice_bitcast_fusion = (bf16[96,2048]{1,0:T(8,128)(2,1)S(1)}, bf16[96,2048]{1,0:T(8,128)(2,1)S(1)}, bf16[96,2048]{1,0:T(8,128)(2,1)S(1)}, bf16[96,2048]...) fusion(bf16[1,256,16384]{2,1,0:T(8,128)(2,1)} %param.3, ...), kind=kLoop, calls=%fused_computation | loop fusion | bytes 6291488 | tf_op jit(solution)/shard_map/dynamic_slice | solution.py:259
  13.9 2.4 %collective-permute-start.3 = (bf16[96,2048]{1,0:T(8,128)(2,1)}, bf16[96,2048]{1,0:T(8,128)(2,1)S(1)}, u32[]{:S(2)}, u32[]{:S(2)}) collective-permute-start(bf16[96,2048]{1,0:T(8,128)(2,1)} %get-tuple-element.26), channel_id=1, source_target_pairs={{0,80},{1,113},{2,82},{3,115},{4,84},{5,117},{6,86},{7,119},{8,88}... | collective-permute-start | bytes 1179656 | tf_op jit(solution)/shard_map/ppermute | solution.py:249
  16.3 0.6 collective-permute-start.2
  16.9 1.5 %collective-permute-start.1 = (bf16[96,2048]{1,0:T(8,128)(2,1)}, bf16[96,2048]{1,0:T(8,128)(2,1)S(1)}, u32[]{:S(2)}, u32[]{:S(2)}) collective-permute-start(bf16[96,2048]{1,0:T(8,128)(2,1)} %get-tuple-element.28), channel_id=1, source_target_pairs={{0,112},{1,81},{2,114},{3,83},{4,116},{5,85},{6,118},{7,87},{8,120... | collective-permute-start | bytes 1179656 | tf_op jit(solution)/shard_map/ppermute | solution.py:249
  18.3 2.1 %collective-permute-start = (bf16[96,2048]{1,0:T(8,128)(2,1)S(1)}, bf16[96,2048]{1,0:T(8,128)(2,1)S(1)}, u32[]{:S(2)}, u32[]{:S(2)}) collective-permute-start(bf16[96,2048]{1,0:T(8,128)(2,1)S(1)} %get-tuple-element.29), channel_id=1, source_target_pairs={{0,16},{1,49},{2,18},{3,51},{4,20},{5,53},{6,22},{7,55},{8,24},{9,... | collective-permute-start | bytes 1179656 | tf_op jit(solution)/shard_map/ppermute | solution.py:249
  20.4 50.8 %all-to-all-done.tasks_same.tasks_other = bf16[8,160,2048]{2,1,0:T(8,128)(2,1)} async-done(((bf16[8,160,2048]{2,1,0:T(8,128)(2,1)}), bf16[8,160,2048]{2,1,0:T(8,128)(2,1)}, u32[]{:S(2)}, u32[]{:S(2)}) %all-to-all-start) | async-done | bytes 5242912 | tf_op jit(solution)/shard_map/all_to_all | solution.py:255
  71.2 6.2 %mean.1 = (bf16[160,1024]{1,0:T(8,128)(2,1)S(1)}, bf16[160,1024]{1,0:T(8,128)(2,1)S(1)}) custom-call(s32[1]{0:T(128)} %bitcast.core, f32[8]{0:T(128)S(1)} %copy-done.1, bf16[8,160,2048]{2,1,0:T(8,128)(2,1)} %all-to-all-done.tasks_same.tasks_other, bf16[8,160,2048]{2,1,0:T(8,128)(2,1)} %all-to-all-done.tasks_same.tasks_other), custom_call_target="tpu_custom_call" | custom-call | tf_op jit(solution)/shard_map/mean/pallas_call | solution.py:141
  77.5 1.6 %collective-permute-start.4 = (bf16[96,2048]{1,0:T(8,128)(2,1)S(1)}, bf16[96,2048]{1,0:T(8,128)(2,1)S(1)}, u32[]{:S(2)}, u32[]{:S(2)}) collective-permute-start(bf16[96,2048]{1,0:T(8,128)(2,1)S(1)} %get-tuple-element.16), channel_id=1, source_target_pairs={{0,48},{1,17},{2,50},{3,19},{4,52},{5,21},{6,54},{7,23},{8,56},{9,... | collective-permute-start | bytes 1179656 | tf_op jit(solution)/shard_map/ppermute | solution.py:249
  79.1 1.3 %collective-permute-start.5 = (bf16[96,2048]{1,0:T(8,128)(2,1)S(1)}, bf16[96,2048]{1,0:T(8,128)(2,1)S(1)}, u32[]{:S(2)}, u32[]{:S(2)}) collective-permute-start(bf16[96,2048]{1,0:T(8,128)(2,1)S(1)} %get-tuple-element.17), channel_id=1, source_target_pairs={{0,96},{1,97},{2,98},{3,99},{4,100},{5,101},{6,102},{7,103},{8,104... | collective-permute-start | bytes 1179656 | tf_op jit(solution)/shard_map/ppermute | solution.py:249
  80.5 6.2 %collective-permute-done.2.refs_3_ = bf16[96,2048]{1,0:T(8,128)(2,1)S(1)} collective-permute-done((bf16[96,2048]{1,0:T(8,128)(2,1)}, bf16[96,2048]{1,0:T(8,128)(2,1)S(1)}, u32[]{:S(2)}, u32[]{:S(2)}) %collective-permute-start.2) | collective-permute-done | bytes 393248 | tf_op jit(solution)/shard_map/ppermute | solution.py:249
  86.7 0.2 collective-permute-done.1.refs_2_
  86.8 4.8 %collective-permute-start.9 = (bf16[160,1024]{1,0:T(8,128)(2,1)S(1)}, bf16[160,1024]{1,0:T(8,128)(2,1)S(1)}, u32[]{:S(2)}, u32[]{:S(2)}) collective-permute-start(bf16[160,1024]{1,0:T(8,128)(2,1)S(1)} %get-tuple-element.21), channel_id=1, source_target_pairs={{0,0},{1,5},{2,22},{3,19},{4,36},{5,33},{6,50},{7,55},{8,64},{9,69... | collective-permute-start | bytes 983048 | tf_op jit(solution)/shard_map/ppermute | solution.py:252
  91.7 15.4 %collective-permute-done.refs_1_ = bf16[96,2048]{1,0:T(8,128)(2,1)S(1)} collective-permute-done((bf16[96,2048]{1,0:T(8,128)(2,1)S(1)}, bf16[96,2048]{1,0:T(8,128)(2,1)S(1)}, u32[]{:S(2)}, u32[]{:S(2)}) %collective-permute-start) | collective-permute-done | bytes 393248 | tf_op jit(solution)/shard_map/ppermute | solution.py:249
  107.1 2.6 %collective-permute-start.10 = (bf16[160,1024]{1,0:T(8,128)(2,1)S(1)}, bf16[160,1024]{1,0:T(8,128)(2,1)S(1)}, u32[]{:S(2)}, u32[]{:S(2)}) collective-permute-start(bf16[160,1024]{1,0:T(8,128)(2,1)S(1)} %get-tuple-element.22), channel_id=1, source_target_pairs={{0,1},{1,4},{2,23},{3,18},{4,37},{5,32},{6,51},{7,54},{8,65},{9,68... | collective-permute-start | bytes 983048 | tf_op jit(solution)/shard_map/ppermute | solution.py:252
  109.7 2.9 %mean_of_blocks.1 = (bf16[96,1024]{1,0:T(8,128)(2,1)S(1)}, bf16[96,1024]{1,0:T(8,128)(2,1)S(1)}) custom-call(f32[8]{0:T(128)S(1)} %copy-done.1, bf16[96,2048]{1,0:T(8,128)(2,1)S(1)} %get-tuple-element.30.refs_0_, bf16[96,2048]{1,0:T(8,128)(2,1)S(1)} %collective-permute-done.refs_1_, bf16[96,2048]{1,0:T(8,128)(2,1)S(1)} %collective-permute-done.1.refs_2_, ...), custom_call_target="tpu_custom_call" | custom-call | tf_op jit(solution)/shard_map/mean_of_blocks/pallas_call | solution.py:179
  112.7 1.9 %collective-permute-start.7 = (bf16[96,1024]{1,0:T(8,128)(2,1)S(1)}, bf16[96,1024]{1,0:T(8,128)(2,1)S(1)}, u32[]{:S(2)}, u32[]{:S(2)}) collective-permute-start(bf16[96,1024]{1,0:T(8,128)(2,1)S(1)} %get-tuple-element.19), channel_id=1, source_target_pairs={{0,0},{1,5},{2,22},{3,19},{4,36},{5,33},{6,50},{7,55},{8,64},{9,69... | collective-permute-start | bytes 589832 | tf_op jit(solution)/shard_map/ppermute | solution.py:252
  114.6 2.8 %collective-permute-start.8 = (bf16[96,1024]{1,0:T(8,128)(2,1)S(1)}, bf16[96,1024]{1,0:T(8,128)(2,1)S(1)}, u32[]{:S(2)}, u32[]{:S(2)}) collective-permute-start(bf16[96,1024]{1,0:T(8,128)(2,1)S(1)} %get-tuple-element.20), channel_id=1, source_target_pairs={{0,1},{1,4},{2,23},{3,18},{4,37},{5,32},{6,51},{7,54},{8,65},{9,68... | collective-permute-start | bytes 589832 | tf_op jit(solution)/shard_map/ppermute | solution.py:252
  117.4 3.9 %collective-permute-done.10.other = bf16[160,1024]{1,0:T(8,128)(2,1)S(1)} collective-permute-done((bf16[160,1024]{1,0:T(8,128)(2,1)S(1)}, bf16[160,1024]{1,0:T(8,128)(2,1)S(1)}, u32[]{:S(2)}, u32[]{:S(2)}) %collective-permute-start.10) | collective-permute-done | bytes 327712 | tf_op jit(solution)/shard_map/ppermute | solution.py:252
  121.3 1.4 %add.182.rest_0_ = f32[512,1024]{1,0:T(8,128)} custom-call(s32[1]{0:T(128)} %bitcast.core, f32[512,1024]{1,0:T(8,128)S(1)} %copy-done, bf16[160,1024]{1,0:T(8,128)(2,1)S(1)} %collective-permute-done.9.same, bf16[160,1024]{1,0:T(8,128)(2,1)S(1)} %collective-permute-done.10.other), custom_call_target="tpu_custom_call" | custom-call | tf_op jit(solution)/shard_map/add/pallas_call | solution.py:225
  122.7 1.8 %collective-permute-done.7.same = bf16[96,1024]{1,0:T(8,128)(2,1)S(1)} collective-permute-done((bf16[96,1024]{1,0:T(8,128)(2,1)S(1)}, bf16[96,1024]{1,0:T(8,128)(2,1)S(1)}, u32[]{:S(2)}, u32[]{:S(2)}) %collective-permute-start.7) | collective-permute-done | bytes 196640 | tf_op jit(solution)/shard_map/ppermute | solution.py:252
  124.5 4.0 %collective-permute-done.8.other = bf16[96,1024]{1,0:T(8,128)(2,1)S(1)} collective-permute-done((bf16[96,1024]{1,0:T(8,128)(2,1)S(1)}, bf16[96,1024]{1,0:T(8,128)(2,1)S(1)}, u32[]{:S(2)}, u32[]{:S(2)}) %collective-permute-start.8) | collective-permute-done | bytes 196640 | tf_op jit(solution)/shard_map/ppermute | solution.py:252
  128.6 1.1 add.183
  (10 shorter events, 0.0 us)
Async XLA Ops:
  4.7 66.5 %all-to-all-start = ((bf16[8,160,2048]{2,1,0:T(8,128)(2,1)}), bf16[8,160,2048]{2,1,0:T(8,128)(2,1)}, u32[]{:S(2)}, u32[]{:S(2)}) async-start(bf16[8,160,2048]{2,1,0:T(8,128)(2,1)} %pack.1), calls=%async_computation | async-start | bytes 10485760 | tf_op jit(solution)/shard_map/all_to_all | solution.py:255
  10.9 60.3 %copy-start.1 = (f32[8]{0:T(128)S(1)}, f32[8]{0:T(128)}, u32[]{:S(2)}) copy-start(f32[8]{0:T(128)} %thresholds.1) | copy-start | bytes 100
  13.9 65.2 %collective-permute-start.3 = (bf16[96,2048]{1,0:T(8,128)(2,1)}, bf16[96,2048]{1,0:T(8,128)(2,1)S(1)}, u32[]{:S(2)}, u32[]{:S(2)}) collective-permute-start(bf16[96,2048]{1,0:T(8,128)(2,1)} %get-tuple-element.26), channel_id=1, source_target_pairs={{0,80},{1,113},{2,82},{3,115},{4,84},{5,117},{6,86},{7,119},{8,88}... | collective-permute-start | bytes 1179656 | tf_op jit(solution)/shard_map/ppermute | solution.py:249
  16.3 70.4 %collective-permute-start.2 = (bf16[96,2048]{1,0:T(8,128)(2,1)}, bf16[96,2048]{1,0:T(8,128)(2,1)S(1)}, u32[]{:S(2)}, u32[]{:S(2)}) collective-permute-start(bf16[96,2048]{1,0:T(8,128)(2,1)} %get-tuple-element.27), channel_id=1, source_target_pairs={{0,32},{1,33},{2,34},{3,35},{4,36},{5,37},{6,38},{7,39},{8,40},{9,... | collective-permute-start | bytes 1179656 | tf_op jit(solution)/shard_map/ppermute | solution.py:249
  16.9 70.0 %collective-permute-start.1 = (bf16[96,2048]{1,0:T(8,128)(2,1)}, bf16[96,2048]{1,0:T(8,128)(2,1)S(1)}, u32[]{:S(2)}, u32[]{:S(2)}) collective-permute-start(bf16[96,2048]{1,0:T(8,128)(2,1)} %get-tuple-element.28), channel_id=1, source_target_pairs={{0,112},{1,81},{2,114},{3,83},{4,116},{5,85},{6,118},{7,87},{8,120... | collective-permute-start | bytes 1179656 | tf_op jit(solution)/shard_map/ppermute | solution.py:249
  18.3 88.7 %collective-permute-start = (bf16[96,2048]{1,0:T(8,128)(2,1)S(1)}, bf16[96,2048]{1,0:T(8,128)(2,1)S(1)}, u32[]{:S(2)}, u32[]{:S(2)}) collective-permute-start(bf16[96,2048]{1,0:T(8,128)(2,1)S(1)} %get-tuple-element.29), channel_id=1, source_target_pairs={{0,16},{1,49},{2,18},{3,51},{4,20},{5,53},{6,22},{7,55},{8,24},{9,... | collective-permute-start | bytes 1179656 | tf_op jit(solution)/shard_map/ppermute | solution.py:249
  71.2 50.1 %copy-start = (f32[512,1024]{1,0:T(8,128)S(1)}, f32[512,1024]{1,0:T(8,128)}, u32[]{:S(2)}) copy-start(f32[512,1024]{1,0:T(8,128)} %base.3) | copy-start | bytes 6291460
  77.5 32.3 %collective-permute-start.4 = (bf16[96,2048]{1,0:T(8,128)(2,1)S(1)}, bf16[96,2048]{1,0:T(8,128)(2,1)S(1)}, u32[]{:S(2)}, u32[]{:S(2)}) collective-permute-start(bf16[96,2048]{1,0:T(8,128)(2,1)S(1)} %get-tuple-element.16), channel_id=1, source_target_pairs={{0,48},{1,17},{2,50},{3,19},{4,52},{5,21},{6,54},{7,23},{8,56},{9,... | collective-permute-start | bytes 1179656 | tf_op jit(solution)/shard_map/ppermute | solution.py:249
  79.1 30.6 %collective-permute-start.5 = (bf16[96,2048]{1,0:T(8,128)(2,1)S(1)}, bf16[96,2048]{1,0:T(8,128)(2,1)S(1)}, u32[]{:S(2)}, u32[]{:S(2)}) collective-permute-start(bf16[96,2048]{1,0:T(8,128)(2,1)S(1)} %get-tuple-element.17), channel_id=1, source_target_pairs={{0,96},{1,97},{2,98},{3,99},{4,100},{5,101},{6,102},{7,103},{8,104... | collective-permute-start | bytes 1179656 | tf_op jit(solution)/shard_map/ppermute | solution.py:249
  86.7 23.1 %collective-permute-start.6 = (bf16[96,2048]{1,0:T(8,128)(2,1)S(1)}, bf16[96,2048]{1,0:T(8,128)(2,1)S(1)}, u32[]{:S(2)}, u32[]{:S(2)}) collective-permute-start(bf16[96,2048]{1,0:T(8,128)(2,1)S(1)} %get-tuple-element.18), channel_id=1, source_target_pairs={{0,64},{1,65},{2,66},{3,67},{4,68},{5,69},{6,70},{7,71},{8,72},{9,... | collective-permute-start | bytes 1179656 | tf_op jit(solution)/shard_map/ppermute | solution.py:249
  86.8 30.6 %collective-permute-start.9 = (bf16[160,1024]{1,0:T(8,128)(2,1)S(1)}, bf16[160,1024]{1,0:T(8,128)(2,1)S(1)}, u32[]{:S(2)}, u32[]{:S(2)}) collective-permute-start(bf16[160,1024]{1,0:T(8,128)(2,1)S(1)} %get-tuple-element.21), channel_id=1, source_target_pairs={{0,0},{1,5},{2,22},{3,19},{4,36},{5,33},{6,50},{7,55},{8,64},{9,69... | collective-permute-start | bytes 983048 | tf_op jit(solution)/shard_map/ppermute | solution.py:252
  107.1 14.2 %collective-permute-start.10 = (bf16[160,1024]{1,0:T(8,128)(2,1)S(1)}, bf16[160,1024]{1,0:T(8,128)(2,1)S(1)}, u32[]{:S(2)}, u32[]{:S(2)}) collective-permute-start(bf16[160,1024]{1,0:T(8,128)(2,1)S(1)} %get-tuple-element.22), channel_id=1, source_target_pairs={{0,1},{1,4},{2,23},{3,18},{4,37},{5,32},{6,51},{7,54},{8,65},{9,68... | collective-permute-start | bytes 983048 | tf_op jit(solution)/shard_map/ppermute | solution.py:252
  112.7 11.9 %collective-permute-start.7 = (bf16[96,1024]{1,0:T(8,128)(2,1)S(1)}, bf16[96,1024]{1,0:T(8,128)(2,1)S(1)}, u32[]{:S(2)}, u32[]{:S(2)}) collective-permute-start(bf16[96,1024]{1,0:T(8,128)(2,1)S(1)} %get-tuple-element.19), channel_id=1, source_target_pairs={{0,0},{1,5},{2,22},{3,19},{4,36},{5,33},{6,50},{7,55},{8,64},{9,69... | collective-permute-start | bytes 589832 | tf_op jit(solution)/shard_map/ppermute | solution.py:252
  114.6 14.0 %collective-permute-start.8 = (bf16[96,1024]{1,0:T(8,128)(2,1)S(1)}, bf16[96,1024]{1,0:T(8,128)(2,1)S(1)}, u32[]{:S(2)}, u32[]{:S(2)}) collective-permute-start(bf16[96,1024]{1,0:T(8,128)(2,1)S(1)} %get-tuple-element.20), channel_id=1, source_target_pairs={{0,1},{1,4},{2,23},{3,18},{4,37},{5,32},{6,51},{7,54},{8,65},{9,68... | collective-permute-start | bytes 589832 | tf_op jit(solution)/shard_map/ppermute | solution.py:252
